TPU v7x, 32 devices: a whole 2x2x4 slice. The times are simulated.
32 devices in a mesh: batch: 4 (over y, x), ctx: 8 (over z, core).
Axes of the slice: x: 2, y: 2, z: 4, core: 2. Of those that a mesh axis runs over, the one named last changes fastest.
Arguments:
- inputs: bfloat16 [4, 1024, 1024], P('batch', 'ctx'), may hold values from -6 to 6
- segments: int32 [4, 1024], P('batch', 'ctx'), may hold values from 0 to 3, never falling along the last dimension, each value on 1 to 512 neighbouring positions
- routes: int32 [4, 1024, 8], P('batch', 'ctx'), may hold values from 0 to 31, all different within a row; in each aligned block of 128 rows (0 to 127, 128 to 255, ..., all dimensions but the last counted through in order) at most 48 rows name the same one
- cotangent: bfloat16 [4, 1024, 1024], P('batch', 'ctx'), may hold values from -6 to 6
- w_query: bfloat16 [1024, 1024], P(('batch', 'ctx')), may hold values from -0.1875 to 0.1875
- w_key: bfloat16 [1024, 512], P(('batch', 'ctx')), may hold values from -0.1875 to 0.1875
- w_value: bfloat16 [1024, 512], P(('batch', 'ctx')), may hold values from -0.1875 to 0.1875
- w_output: bfloat16 [1024, 1024], P(('batch', 'ctx')), may hold values from -0.75 to 0.75
- w_router: bfloat16 [1024, 32], P(('batch', 'ctx')), may hold values from -0.5 to 0.5
- norm_attn: bfloat16 [1024], P(('batch', 'ctx')), may hold values from 0.5 to 1.5
- norm_moe: bfloat16 [1024], P(('batch', 'ctx')), may hold values from 0.5 to 1.5
- w_gate: bfloat16 [32, 1024, 512], P('ctx', 'batch'), may hold values from -0.1875 to 0.1875
- w_up: bfloat16 [32, 1024, 512], P('ctx', 'batch'), may hold values from -0.1875 to 0.1875
- w_down: bfloat16 [32, 1024, 512], P('ctx', 'batch'), may hold values from -0.25 to 0.25
Outputs:
- block_out: bfloat16 [4, 1024, 1024], P('batch', 'ctx')
- grad_inputs: float32 [4, 1024, 1024], P('batch', 'ctx')
- grad_w_query: float32 [1024, 1024], P(('batch', 'ctx'))
- grad_w_key: float32 [1024, 512], P(('batch', 'ctx'))
- grad_w_value: float32 [1024, 512], P(('batch', 'ctx'))
- grad_w_output: float32 [1024, 1024], P(('batch', 'ctx'))
- grad_w_router: float32 [1024, 32], P(('batch', 'ctx'))
- grad_norm_attn: float32 [1024], P(('batch', 'ctx'))
- grad_norm_moe: float32 [1024], P(('batch', 'ctx'))
- grad_w_gate: float32 [32, 1024, 512], P('ctx', 'batch')
- grad_w_up: float32 [32, 1024, 512], P('ctx', 'batch')
- grad_w_down: float32 [32, 1024, 512], P('ctx', 'batch')
Inputs may be any that keep to these rules, and one draw needn't show every extreme that they name: `routes`: each token names 8 different experts. Among the 128 tokens of one device (aligned blocks of the token order), no expert is named more than 48 times, and in some blocks some expert exactly 48 times. `segments`: documents are numbered from 0 along each sequence, never falling; a document has at most half of 1024 tokens, and some document is exactly that long.
All inputs are finite; a program needn't handle non-finite values.
Results may differ from a plain program's by a relative error of at most 0.018.
Values may be sent and summed in bfloat16 or wider, within the bound.
A program may use at most 192 MiB of HBM per device.

v0:
```python
import math

import jax
import jax.numpy as jnp
from jax import lax
from jax.sharding import PartitionSpec as P

HEADS = 16
KV_HEADS = 8
HEAD_DIM = 64
EXPERTS = 32
CAP = 48


EPS = 1e-06
ROPE_BASE = 10000.0


def rope_tables(positions, head_size):
    half_size = head_size // 2
    exponent = jnp.arange(half_size, dtype=jnp.float32) * (2.0 / head_size)
    inverse = jnp.exp(-exponent * math.log(ROPE_BASE))
    angles = positions.astype(jnp.float32)[:, None] * inverse[None, :]
    return (jnp.cos(angles), jnp.sin(angles))


def rotate(values, cos_table, sin_table):
    half_size = values.shape[-1] // 2
    lower_half = values[..., :half_size]
    upper_half = values[..., half_size:]
    cos_part = cos_table[:, None, :]
    sin_part = sin_table[:, None, :]
    return jnp.concatenate(
        [
            lower_half * cos_part - upper_half * sin_part,
            upper_half * cos_part + lower_half * sin_part,
        ],
        axis=-1,
    )


def route_slots(route_ids, experts, capacity):
    flat_ids = route_ids.reshape(-1)
    chosen = (flat_ids[:, None] == jnp.arange(experts, dtype=jnp.int32)[None, :]).astype(jnp.int32)
    earlier = jnp.cumsum(chosen, axis=0) - chosen
    return flat_ids * capacity + jnp.sum(earlier * chosen, axis=1)


def attend(queries, key_rows, value_rows, allowed, score_scale):
    scores = (
        jnp.einsum("tkgd,skd->kgts", queries, key_rows, preferred_element_type=jnp.float32)
        * score_scale
    )
    exp_scores = jnp.where(allowed[None, None], jnp.exp(scores), 0.0)
    totals = jnp.sum(exp_scores, axis=-1, keepdims=True)
    prob_wire = (exp_scores / totals).astype(jnp.bfloat16)
    output = jnp.einsum("kgts,skd->tkgd", prob_wire, value_rows, preferred_element_type=jnp.float32)
    return (output.astype(jnp.bfloat16), jnp.log(totals))


def score_grads(
    queries, key_rows, value_rows, allowed, score_scale, log_totals, delta_heads, grad_rows
):
    scores = (
        jnp.einsum("tkgd,skd->kgts", queries, key_rows, preferred_element_type=jnp.float32)
        * score_scale
    )
    prob_again = jnp.where(allowed[None, None], jnp.exp(scores - log_totals), 0.0)
    grad_prob = jnp.einsum(
        "tkgd,skd->kgts", grad_rows, value_rows, preferred_element_type=jnp.float32
    )
    grad_score = (prob_again * (grad_prob - delta_heads) * score_scale).astype(jnp.bfloat16)
    return (prob_again.astype(jnp.bfloat16), grad_score)


def shards(
    inputs,
    segments,
    routes,
    cotangent,
    w_query,
    w_key,
    w_value,
    w_output,
    w_router,
    norm_attn,
    norm_moe,
    w_gate,
    w_up,
    w_down,
):
    tok_rows = inputs.shape[1]
    model_width = inputs.shape[2]
    top_count = routes.shape[2]
    ctx_count = lax.axis_size("ctx")
    ctx_index = lax.axis_index("ctx")
    seq_length = tok_rows * ctx_count
    groups_per = HEADS // KV_HEADS
    kv_width = KV_HEADS * HEAD_DIM
    query_width = HEADS * HEAD_DIM
    slot_total = EXPERTS * CAP
    score_scale = 1.0 / math.sqrt(HEAD_DIM)
    residual_in = inputs[0].astype(jnp.float32)
    seg_local = segments[0]
    route_local = routes[0]
    grad_wire = cotangent[0]
    grad_out = grad_wire.astype(jnp.float32)
    positions = ctx_index * tok_rows + jnp.arange(tok_rows, dtype=jnp.int32)
    cos_table, sin_table = rope_tables(positions, HEAD_DIM)
    dense_held = (
        lax.all_gather(w_query, ("batch", "ctx"), axis=0, tiled=True),
        lax.all_gather(w_key, ("batch", "ctx"), axis=0, tiled=True),
        lax.all_gather(w_value, ("batch", "ctx"), axis=0, tiled=True),
        lax.all_gather(w_output, ("batch", "ctx"), axis=0, tiled=True),
        lax.all_gather(w_router, ("batch", "ctx"), axis=0, tiled=True),
        lax.all_gather(norm_attn, ("batch", "ctx"), axis=0, tiled=True),
        lax.all_gather(norm_moe, ("batch", "ctx"), axis=0, tiled=True),
    )
    experts_held = (
        lax.all_gather(w_gate, "batch", axis=1, tiled=True),
        lax.all_gather(w_up, "batch", axis=1, tiled=True),
        lax.all_gather(w_down, "batch", axis=1, tiled=True),
    )
    query_full, key_full, value_full, output_full, router_full, gain_attn, gain_moe = dense_held
    gate_full, up_full, down_full = experts_held
    local_experts = gate_full.shape[0]
    inv_first = lax.rsqrt(jnp.mean(residual_in * residual_in, axis=-1, keepdims=True) + EPS)
    normed_attn = (residual_in * inv_first * gain_attn.astype(jnp.float32)).astype(jnp.bfloat16)
    query_proj = jnp.dot(normed_attn, query_full, preferred_element_type=jnp.float32)
    key_proj = jnp.dot(normed_attn, key_full, preferred_element_type=jnp.float32)
    value_proj = jnp.dot(normed_attn, value_full, preferred_element_type=jnp.float32)
    query_rot = rotate(query_proj.reshape(tok_rows, HEADS, HEAD_DIM), cos_table, sin_table).astype(
        jnp.bfloat16
    )
    key_rot = rotate(key_proj.reshape(tok_rows, KV_HEADS, HEAD_DIM), cos_table, sin_table).astype(
        jnp.bfloat16
    )
    value_rows = value_proj.astype(jnp.bfloat16)
    seg_wire = seg_local.astype(jnp.bfloat16)
    key_all, value_all, seg_all = (
        lax.all_gather(key_rot.reshape(tok_rows, kv_width), "ctx", axis=0, tiled=True),
        lax.all_gather(value_rows, "ctx", axis=0, tiled=True),
        lax.all_gather(seg_wire, "ctx", axis=0, tiled=True),
    )
    key_pos = jnp.arange(seq_length, dtype=jnp.int32)
    allowed = (seg_wire[:, None] == seg_all[None, :]) & (key_pos[None, :] <= positions[:, None])
    query_groups = query_rot.reshape(tok_rows, KV_HEADS, groups_per, HEAD_DIM)
    key_heads = key_all.reshape(seq_length, KV_HEADS, HEAD_DIM)
    value_heads = value_all.reshape(seq_length, KV_HEADS, HEAD_DIM)
    attn_rows, log_totals = attend(query_groups, key_heads, value_heads, allowed, score_scale)
    attn_flat = attn_rows.reshape(tok_rows, query_width)
    hidden_res = residual_in + jnp.dot(attn_flat, output_full, preferred_element_type=jnp.float32)
    inv_second = lax.rsqrt(jnp.mean(hidden_res * hidden_res, axis=-1, keepdims=True) + EPS)
    normed_moe = (hidden_res * inv_second * gain_moe.astype(jnp.float32)).astype(jnp.bfloat16)
    logits = jnp.dot(normed_moe, router_full, preferred_element_type=jnp.float32)
    route_hot = (
        route_local[:, :, None] == jnp.arange(EXPERTS, dtype=jnp.int32)[None, None, :]
    ).astype(jnp.float32)
    chosen_logits = jnp.sum(route_hot * logits[:, None, :], axis=-1)
    route_exp = jnp.exp(chosen_logits)
    route_weights = route_exp / jnp.sum(route_exp, axis=-1, keepdims=True)
    slot_rows = route_slots(route_local, EXPERTS, CAP)
    slot_ids = jnp.arange(slot_total, dtype=jnp.int32)
    dispatch = jnp.any(
        slot_rows.reshape(tok_rows, top_count)[:, :, None] == slot_ids[None, None, :], axis=1
    ).astype(jnp.bfloat16)
    send_rows = (
        jnp.einsum("tj,td->jd", dispatch, normed_moe, preferred_element_type=jnp.float32)
        .astype(jnp.bfloat16)
        .reshape(EXPERTS, CAP, model_width)
    )
    arrived_rows = lax.all_to_all(send_rows, "ctx", split_axis=0, concat_axis=0, tiled=True)
    slot_count = arrived_rows.shape[1]
    grouped = arrived_rows.reshape(-1, local_experts, slot_count, model_width)
    gate_act = jnp.einsum("gesd,edf->gesf", grouped, gate_full, preferred_element_type=jnp.float32)
    up_act = jnp.einsum("gesd,edf->gesf", grouped, up_full, preferred_element_type=jnp.float32)
    hidden_act = (gate_act * jax.nn.sigmoid(gate_act) * up_act).astype(jnp.bfloat16)
    expert_out = jnp.einsum(
        "gesf,edf->gesd", hidden_act, down_full, preferred_element_type=jnp.float32
    ).astype(jnp.bfloat16)
    sent_back = lax.all_to_all(
        expert_out.reshape(arrived_rows.shape), "ctx", split_axis=0, concat_axis=0, tiled=True
    )
    unit_count = gate_act.shape[-1]
    gate_pre = gate_act.reshape(-1, slot_count, unit_count)
    up_pre = up_act.reshape(-1, slot_count, unit_count)
    picked = (
        sent_back.reshape(slot_total, model_width)[slot_rows]
        .reshape(tok_rows, top_count, model_width)
        .astype(jnp.float32)
    )
    moe_out = jnp.sum(route_weights[:, :, None] * picked, axis=1)
    block_out = (hidden_res + moe_out).astype(jnp.bfloat16)
    dense_back = (
        lax.all_gather(w_query, ("batch", "ctx"), axis=0, tiled=True),
        lax.all_gather(w_key, ("batch", "ctx"), axis=0, tiled=True),
        lax.all_gather(w_value, ("batch", "ctx"), axis=0, tiled=True),
        lax.all_gather(w_output, ("batch", "ctx"), axis=0, tiled=True),
        lax.all_gather(w_router, ("batch", "ctx"), axis=0, tiled=True),
        lax.all_gather(norm_attn, ("batch", "ctx"), axis=0, tiled=True),
        lax.all_gather(norm_moe, ("batch", "ctx"), axis=0, tiled=True),
    )
    experts_back = (
        lax.all_gather(w_gate, "batch", axis=1, tiled=True),
        lax.all_gather(w_up, "batch", axis=1, tiled=True),
        lax.all_gather(w_down, "batch", axis=1, tiled=True),
    )
    query_back, key_back, value_back, output_back, router_back, gain_attn_back, gain_moe_back = (
        dense_back
    )
    gate_back, up_back, down_back = experts_back
    grad_weights = jnp.sum(grad_out[:, None, :] * picked, axis=-1)
    grad_chosen = route_weights * (
        grad_weights - jnp.sum(route_weights * grad_weights, axis=-1, keepdims=True)
    )
    grad_logits = jnp.sum(route_hot * grad_chosen[:, :, None], axis=1).astype(jnp.bfloat16)
    grad_router = jnp.dot(normed_moe.T, grad_logits, preferred_element_type=jnp.float32)
    grad_normed = jnp.dot(grad_logits, router_back.T, preferred_element_type=jnp.float32)
    slot_weight = jnp.zeros((slot_total,), jnp.float32).at[slot_rows].set(route_weights.reshape(-1))
    grad_gathered = jnp.einsum("tj,td->jd", dispatch, grad_wire, preferred_element_type=jnp.float32)
    grad_send = (
        (slot_weight[:, None] * grad_gathered)
        .astype(jnp.bfloat16)
        .reshape(EXPERTS, CAP, model_width)
    )
    grad_arrived = lax.all_to_all(grad_send, "ctx", split_axis=0, concat_axis=0, tiled=True)
    unit_count = gate_pre.shape[-1]
    grad_group = grad_arrived.reshape(-1, local_experts, CAP, model_width)
    arrived_group = arrived_rows.reshape(-1, local_experts, CAP, model_width)
    gate_group = gate_pre.reshape(-1, local_experts, CAP, unit_count)
    up_group = up_pre.reshape(-1, local_experts, CAP, unit_count)
    grad_hidden = jnp.einsum(
        "gesd,edf->gesf", grad_group, down_back, preferred_element_type=jnp.float32
    )
    sigmoid_gate = jax.nn.sigmoid(gate_group)
    silu_gate = gate_group * sigmoid_gate
    hidden_again = (silu_gate * up_group).astype(jnp.bfloat16)
    grad_gate = (
        grad_hidden * up_group * sigmoid_gate * (1.0 + gate_group * (1.0 - sigmoid_gate))
    ).astype(jnp.bfloat16)
    grad_up = (grad_hidden * silu_gate).astype(jnp.bfloat16)
    grad_expert_in = (
        jnp.einsum("gesf,edf->gesd", grad_gate, gate_back, preferred_element_type=jnp.float32)
        + jnp.einsum("gesf,edf->gesd", grad_up, up_back, preferred_element_type=jnp.float32)
    ).astype(jnp.bfloat16)
    grad_w_gate = jnp.einsum(
        "gesd,gesf->edf", arrived_group, grad_gate, preferred_element_type=jnp.float32
    )
    grad_w_up = jnp.einsum(
        "gesd,gesf->edf", arrived_group, grad_up, preferred_element_type=jnp.float32
    )
    grad_w_down = jnp.einsum(
        "gesd,gesf->edf", grad_group, hidden_again, preferred_element_type=jnp.float32
    )
    grad_back = lax.all_to_all(
        grad_expert_in.reshape(EXPERTS, CAP, model_width),
        "ctx",
        split_axis=0,
        concat_axis=0,
        tiled=True,
    )
    gate_sum, up_sum, down_sum = (
        lax.psum_scatter(
            grad_w_gate.astype(jnp.bfloat16), "batch", scatter_dimension=1, tiled=True
        ).astype(jnp.float32),
        lax.psum_scatter(
            grad_w_up.astype(jnp.bfloat16), "batch", scatter_dimension=1, tiled=True
        ).astype(jnp.float32),
        lax.psum_scatter(
            grad_w_down.astype(jnp.bfloat16), "batch", scatter_dimension=1, tiled=True
        ).astype(jnp.float32),
    )
    grad_picked = (
        grad_back.reshape(slot_total, model_width)[slot_rows]
        .reshape(tok_rows, top_count, model_width)
        .astype(jnp.float32)
    )
    grad_normed = grad_normed + jnp.sum(grad_picked, axis=1)
    gain_moe_wide = gain_moe_back.astype(jnp.float32)
    gained_moe = grad_normed * gain_moe_wide
    grad_gain_moe = jnp.sum(grad_normed * hidden_res * inv_second, axis=0)
    grad_hidden_res = (
        grad_out
        + inv_second * gained_moe
        - hidden_res * inv_second**3 * jnp.mean(gained_moe * hidden_res, axis=-1, keepdims=True)
    )
    grad_attn = grad_hidden_res.astype(jnp.bfloat16)
    grad_w_output = jnp.dot(attn_flat.T, grad_attn, preferred_element_type=jnp.float32)
    grad_attn_rows = (
        jnp.dot(grad_attn, output_back.T, preferred_element_type=jnp.float32)
        .astype(jnp.bfloat16)
        .reshape(tok_rows, KV_HEADS, groups_per, HEAD_DIM)
    )
    delta_rows = jnp.sum(
        grad_attn_rows.astype(jnp.float32) * attn_rows.astype(jnp.float32), axis=-1
    )
    prob_wire, grad_score = score_grads(
        query_groups,
        key_heads,
        value_heads,
        allowed,
        score_scale,
        log_totals,
        jnp.transpose(delta_rows, (1, 2, 0))[..., None],
        grad_attn_rows,
    )
    grad_query_rot = jnp.einsum(
        "kgts,skd->tkgd", grad_score, key_heads, preferred_element_type=jnp.float32
    )
    query_all, grad_rows_all = (
        lax.all_gather(query_rot.reshape(tok_rows, query_width), "ctx", axis=0, tiled=True),
        lax.all_gather(grad_attn_rows.reshape(tok_rows, query_width), "ctx", axis=0, tiled=True),
    )
    log_all, delta_all = (
        lax.all_gather(jnp.transpose(log_totals[..., 0], (2, 0, 1)), "ctx", axis=0, tiled=True),
        lax.all_gather(delta_rows, "ctx", axis=0, tiled=True),
    )
    query_seq = query_all.reshape(seq_length, KV_HEADS, groups_per, HEAD_DIM)
    grad_seq = grad_rows_all.reshape(seq_length, KV_HEADS, groups_per, HEAD_DIM)
    allowed_keys = (seg_all[:, None] == seg_wire[None, :]) & (
        positions[None, :] <= key_pos[:, None]
    )
    prob_keys, score_keys = score_grads(
        query_seq,
        key_rot,
        value_rows.reshape(tok_rows, KV_HEADS, HEAD_DIM),
        allowed_keys,
        score_scale,
        jnp.transpose(log_all, (1, 2, 0))[..., None],
        jnp.transpose(delta_all, (1, 2, 0))[..., None],
        grad_seq,
    )
    grad_key_own = jnp.einsum(
        "kgts,tkgd->skd", score_keys, query_seq, preferred_element_type=jnp.float32
    )
    grad_value_own = jnp.einsum(
        "kgts,tkgd->skd", prob_keys, grad_seq, preferred_element_type=jnp.float32
    )
    kv_mine = jnp.concatenate(
        [grad_key_own.reshape(tok_rows, kv_width), grad_value_own.reshape(tok_rows, kv_width)],
        axis=1,
    )
    grad_query = (
        rotate(grad_query_rot.reshape(tok_rows, HEADS, HEAD_DIM), cos_table, -sin_table)
        .reshape(tok_rows, query_width)
        .astype(jnp.bfloat16)
    )
    grad_key = (
        rotate(kv_mine[:, :kv_width].reshape(tok_rows, KV_HEADS, HEAD_DIM), cos_table, -sin_table)
        .reshape(tok_rows, kv_width)
        .astype(jnp.bfloat16)
    )
    grad_value = kv_mine[:, kv_width:].astype(jnp.bfloat16)
    grad_w_query = jnp.dot(normed_attn.T, grad_query, preferred_element_type=jnp.float32)
    grad_w_key = jnp.dot(normed_attn.T, grad_key, preferred_element_type=jnp.float32)
    grad_w_value = jnp.dot(normed_attn.T, grad_value, preferred_element_type=jnp.float32)
    grad_normed_attn = (
        jnp.dot(grad_query, query_back.T, preferred_element_type=jnp.float32)
        + jnp.dot(grad_key, key_back.T, preferred_element_type=jnp.float32)
        + jnp.dot(grad_value, value_back.T, preferred_element_type=jnp.float32)
    )
    gained_attn = grad_normed_attn * gain_attn_back.astype(jnp.float32)
    grad_gain_attn = jnp.sum(grad_normed_attn * residual_in * inv_first, axis=0)
    grad_inputs = (
        grad_hidden_res
        + inv_first * gained_attn
        - residual_in * inv_first**3 * jnp.mean(gained_attn * residual_in, axis=-1, keepdims=True)
    )
    query_sum, key_sum, value_sum, output_sum, router_sum, attn_gain_sum, moe_gain_sum = (
        lax.psum_scatter(grad_w_query, ("batch", "ctx"), scatter_dimension=0, tiled=True),
        lax.psum_scatter(grad_w_key, ("batch", "ctx"), scatter_dimension=0, tiled=True),
        lax.psum_scatter(grad_w_value, ("batch", "ctx"), scatter_dimension=0, tiled=True),
        lax.psum_scatter(grad_w_output, ("batch", "ctx"), scatter_dimension=0, tiled=True),
        lax.psum_scatter(grad_router, ("batch", "ctx"), scatter_dimension=0, tiled=True),
        lax.psum_scatter(grad_gain_attn, ("batch", "ctx"), scatter_dimension=0, tiled=True),
        lax.psum_scatter(grad_gain_moe, ("batch", "ctx"), scatter_dimension=0, tiled=True),
    )
    return (
        block_out[None],
        grad_inputs[None],
        query_sum,
        key_sum,
        value_sum,
        output_sum,
        router_sum,
        attn_gain_sum,
        moe_gain_sum,
        gate_sum,
        up_sum,
        down_sum,
    )


def solution(mesh):
    placed = (
        P("batch", "ctx", None),
        P("batch", "ctx"),
        P("batch", "ctx", None),
        P("batch", "ctx", None),
        P(("batch", "ctx"), None),
        P(("batch", "ctx"), None),
        P(("batch", "ctx"), None),
        P(("batch", "ctx"), None),
        P(("batch", "ctx"), None),
        P(("batch", "ctx")),
        P(("batch", "ctx")),
        P("ctx", "batch", None),
        P("ctx", "batch", None),
        P("ctx", "batch", None),
    )
    return jax.shard_map(
        shards,
        mesh=mesh,
        in_specs=placed,
        out_specs=(
            P("batch", "ctx", None),
            P("batch", "ctx", None),
            P(("batch", "ctx"), None),
            P(("batch", "ctx"), None),
            P(("batch", "ctx"), None),
            P(("batch", "ctx"), None),
            P(("batch", "ctx"), None),
            P(("batch", "ctx")),
            P(("batch", "ctx")),
            P("ctx", "batch", None),
            P("ctx", "batch", None),
            P("ctx", "batch", None),
        ),
        check_vma=False,
    )
```

profile of v0, /device:TPU:0, one launch (start us, length us, event | category | flops | bytes accessed | tf_op | source)
XLA Modules:
  0.0 1578.6 jit_solution(15883958956908626011)
XLA Ops:
  10.4 42.0 %all-reduce.5 = (bf16[1024]{0:T(1024)(128)(2,1)S(1)}, bf16[1024]{0:T(1024)(128)(2,1)S(1)}) all-reduce(bf16[1024]{0:T(1024)(128)(2,1)S(1)} %dynamic-update-slice, bf16[1024]{0:T(1024)(128)(2,1)S(1)} %dynamic-update-slice.1), channel_id=1, replica_groups=mesh['batch'=4,'ctx'=8] {'batch','ctx'}, use_global_device_ids=true, to_apply=%add | all-reduce | flops 2048 | bytes 8192
  54.0 13.6 all-gather.13.cloned.1.call-done
  71.3 52.1 %all-gather.17.cloned.1.call-done = bf16[1024,512]{1,0:T(8,128)(2,1)} async-done(((bf16[32,512]{1,0:T(8,128)(2,1)}), bf16[1024,512]{1,0:T(8,128)(2,1)}) %all-gather.17.cloned.1.call-update) | async-done | bytes 1048592 | tf_op jit(solution)/shard_map/all_gather | solution.py:112
  128.6 11.2 all-gather
  139.9 9.0 reduce-window.6
  155.2 50.7 %all-gather.21.cloned.1.call-done = bf16[1024,1024]{1,0:T(8,128)(2,1)} async-done(((bf16[32,1024]{1,0:T(8,128)(2,1)}), bf16[1024,1024]{1,0:T(8,128)(2,1)}) %all-gather.21.cloned.1.call-update) | async-done | bytes 2097168 | tf_op jit(solution)/shard_map/all_gather | solution.py:111
  209.8 21.0 %all-gather.19.cloned.1.call-done = bf16[1024,512]{0,1:T(8,128)(2,1)} async-done(((bf16[128,512]{0,1:T(8,128)(2,1)}), bf16[1024,512]{0,1:T(8,128)(2,1)}) %all-gather.19.cloned.1.call-update) | async-done | bytes 1048592 | tf_op jit(solution)/shard_map/all_gather | solution.py:141
  239.2 49.6 %all-gather.23.cloned.1.call-done = bf16[1024,1024]{1,0:T(8,128)(2,1)} async-done(((bf16[32,1024]{1,0:T(8,128)(2,1)}), bf16[1024,1024]{1,0:T(8,128)(2,1)}) %all-gather.23.cloned.1.call-update) | async-done | bytes 2097168 | tf_op jit(solution)/shard_map/all_gather | solution.py:114
  300.1 101.4 %all_gather.70 = bf16[1024,32]{1,0:T(8,128)(2,1)S(1)} all-gather(bf16[32,32]{1,0:T(8,128)(2,1)S(1)} %copy-done.61), channel_id=1, replica_groups=mesh['batch'=4,'ctx'=8] {'batch','ctx'}, dimensions={0}, use_global_device_ids=true | all-gather | bytes 67584 | tf_op jit(solution)/shard_map/all_gather | solution.py:115
  413.2 6.6 fusion.22
  419.8 6.7 fusion.18
  426.5 25.5 %all-gather.29.cloned.1.call-done = bf16[4,1024,512]{2,1,0:T(8,128)(2,1)} async-done(((bf16[4,256,512]{2,1,0:T(8,128)(2,1)}), bf16[4,1024,512]{2,1,0:T(8,128)(2,1)}) %all-gather.29.cloned.1.call-update) | async-done | bytes 4194320 | tf_op jit(solution)/shard_map/all_gather | solution.py:122
  452.0 32.6 %all-to-all-done.2 = bf16[32,48,1024]{2,1,0:T(8,128)(2,1)S(1)} async-done(((bf16[32,48,1024]{2,1,0:T(8,128)(2,1)}), bf16[32,48,1024]{2,1,0:T(8,128)(2,1)S(1)}, u32[]{:S(2)}, u32[]{:S(2)}) %all-to-all-start.2) | async-done | bytes 3145760 | tf_op jit(solution)/shard_map/all_to_all | solution.py:226
  484.6 8.3 fusion.45
  509.1 62.8 %all-to-all-done.1 = bf16[32,48,1024]{2,1,0:T(8,128)(2,1)S(1)} async-done(((bf16[32,48,1024]{2,1,0:T(8,128)(2,1)}), bf16[32,48,1024]{2,1,0:T(8,128)(2,1)S(1)}, u32[]{:S(2)}, u32[]{:S(2)}) %all-to-all-start.1) | async-done | bytes 3145760 | tf_op jit(solution)/shard_map/all_to_all | solution.py:181
  591.3 73.4 %all-to-all-done.3 = bf16[32,48,1024]{2,1,0:T(8,128)(2,1)} async-done(((bf16[32,48,1024]{2,1,0:T(8,128)(2,1)}), bf16[32,48,1024]{2,1,0:T(8,128)(2,1)}, u32[]{:S(2)}, u32[]{:S(2)}) %all-to-all-start.3) | async-done | bytes 3145760 | tf_op jit(solution)/shard_map/all_to_all | solution.py:255
  664.8 7.3 gather_fusion.1
  677.3 6.3 bitcast_convert_fusion
  685.0 6.3 bitcast_convert_fusion.2
  692.8 6.4 bitcast_convert_fusion.1
  700.7 10.2 all_gather.75
  733.1 9.2 all_gather.77
  742.3 9.7 fusion.63
  759.1 7.1 fusion.32
  775.3 40.0 %reduce-scatter.19.cloned.1.call-done = bf16[4,256,512]{2,1,0:T(8,128)(2,1)} async-done(((bf16[4,1024,512]{2,1,0:T(8,128)(2,1)}), bf16[4,256,512]{2,1,0:T(8,128)(2,1)}) %reduce-scatter.19.cloned.1.call-update) | async-done | bytes 1048592 | tf_op jit(solution)/shard_map/reduce_scatter | solution.py:263
  818.2 52.6 %reduce-scatter.21.cloned.1.call-done = bf16[4,256,512]{2,1,0:T(8,128)(2,1)} async-done(((bf16[4,1024,512]{2,1,0:T(8,128)(2,1)}), bf16[4,256,512]{2,1,0:T(8,128)(2,1)}) %reduce-scatter.21.cloned.1.call-update) | async-done | bytes 1048592 | tf_op jit(solution)/shard_map/reduce_scatter | solution.py:266
  874.8 39.4 %all-reduce.4 = (f32[1024]{0:T(1024)S(1)}, f32[1024]{0:T(1024)S(1)}) all-reduce(f32[1024]{0:T(1024)S(1)} %get-tuple-element.16, f32[1024]{0:T(1024)S(1)} %copy-done.59), channel_id=8, replica_groups=mesh['batch'=4,'ctx'=8] {'batch','ctx'}, use_global_device_ids=true, to_apply=%region_24.25.clone | all-reduce | flops 2048 | bytes 16384
  916.4 92.9 %reduce-scatter.17.cloned.1.call-done = f32[32,32]{1,0:T(8,128)} async-done(((f32[1024,32]{1,0:T(8,128)}), f32[32,32]{1,0:T(8,128)}) %reduce-scatter.17.cloned.1.call-update) | async-done | bytes 4112 | tf_op jit(solution)/shard_map/reduce_scatter | solution.py:374
  1009.2 137.9 %reduce-scatter.13.cloned.1.call-done = f32[32,512]{1,0:T(8,128)} async-done(((f32[1024,512]{1,0:T(8,128)}), f32[32,512]{1,0:T(8,128)}) %reduce-scatter.13.cloned.1.call-update) | async-done | bytes 65552 | tf_op jit(solution)/shard_map/reduce_scatter | solution.py:372
  1147.1 138.0 %reduce-scatter.11.cloned.1.call-done = f32[32,512]{1,0:T(8,128)} async-done(((f32[1024,512]{1,0:T(8,128)}), f32[32,512]{1,0:T(8,128)}) %reduce-scatter.11.cloned.1.call-update) | async-done | bytes 65552 | tf_op jit(solution)/shard_map/reduce_scatter | solution.py:371
  1285.1 143.6 %reduce-scatter.15.cloned.1.call-done = f32[32,1024]{1,0:T(8,128)} async-done(((f32[1024,1024]{1,0:T(8,128)}), f32[32,1024]{1,0:T(8,128)}) %reduce-scatter.15.cloned.1.call-update) | async-done | bytes 131088 | tf_op jit(solution)/shard_map/reduce_scatter | solution.py:373
  1428.7 143.1 %reduce-scatter.9.cloned.1.call-done = f32[32,1024]{1,0:T(8,128)} async-done(((f32[1024,1024]{1,0:T(8,128)}), f32[32,1024]{1,0:T(8,128)}) %reduce-scatter.9.cloned.1.call-update) | async-done | bytes 131088 | tf_op jit(solution)/shard_map/reduce_scatter | solution.py:370
  (313 shorter events, 146.8 us)
Async XLA Ops:
  7.2 117.8 %copy-start = (bf16[1,128,1024]{2,1,0:T(8,128)(2,1)S(1)}, bf16[1,128,1024]{2,1,0:T(8,128)(2,1)}, u32[]{:S(2)}) copy-start(bf16[1,128,1024]{2,1,0:T(8,128)(2,1)} %param.14) | copy-start | bytes 786436
  7.2 60.4 %all-gather.13.cloned.1.call-start = ((), (), s32[]{:S(2)}) async-start(), calls=%async_computation.12 | async-start | bytes 1081344 | tf_op jit(solution)/shard_map/all_gather | solution.py:113
  7.9 115.5 %all-gather.17.cloned.1.call-start = ((), (), s32[]{:S(2)}) async-start(), calls=%async_computation.14 | async-start | bytes 1081344 | tf_op jit(solution)/shard_map/all_gather | solution.py:112
  8.7 144.3 %all-gather.15.cloned.1.call-start = ((), (), s32[]{:S(2)}) async-start(), calls=%async_computation.13 | async-start | bytes 1179648 | tf_op jit(solution)/shard_map/all_gather | solution.py:142
  52.4 156.4 %copy-start.34 = (f32[1024]{0:T(1024)}, f32[1024]{0:T(1024)S(1)}, u32[]{:S(2)}) copy-start(f32[1024]{0:T(1024)S(1)} %convert_element_type.223) | copy-start | bytes 12292
  54.0 154.8 %copy-start.53 = (f32[128]{0:T(128)}, f32[128]{0:T(128)S(1)}, u32[]{:S(2)}) copy-start(f32[128]{0:T(128)S(1)} %get-tuple-element.41) | copy-start | bytes 1540
  69.9 136.0 %all-gather.21.cloned.1.call-start = ((), (), s32[]{:S(2)}) async-start(), calls=%async_computation.16 | async-start | bytes 2162688 | tf_op jit(solution)/shard_map/all_gather | solution.py:111
  70.5 160.2 %all-gather.19.cloned.1.call-start = ((), (), s32[]{:S(2)}) async-start(), calls=%async_computation.15 | async-start | bytes 1179648 | tf_op jit(solution)/shard_map/all_gather | solution.py:141
  126.2 162.5 %all-gather.23.cloned.1.call-start = ((), (), s32[]{:S(2)}) async-start(), calls=%async_computation.17 | async-start | bytes 2162688 | tf_op jit(solution)/shard_map/all_gather | solution.py:114
  126.8 286.4 %all-gather.25.cloned.1.call-start = ((), (), s32[]{:S(2)}) async-start(), calls=%async_computation.18 | async-start | bytes 5242880 | tf_op jit(solution)/shard_map/all_gather | solution.py:120
  127.5 292.3 %all-gather.27.cloned.1.call-start = ((), (), s32[]{:S(2)}) async-start(), calls=%async_computation.19 | async-start | bytes 5242880 | tf_op jit(solution)/shard_map/all_gather | solution.py:121
  139.9 151.6 %copy-start.46 = (f32[1024]{0:T(1024)}, f32[1024]{0:T(1024)S(1)}, u32[]{:S(2)}) copy-start(f32[1024]{0:T(1024)S(1)} %convert_element_type.237) | copy-start | bytes 12292
  152.9 81.1 %copy-start.39 = (pred[128,1024]{0,1:T(8,128)(4,1)}, pred[128,1024]{0,1:T(8,128)(4,1)S(1)}, u32[]{:S(2)}) copy-start(pred[128,1024]{0,1:T(8,128)(4,1)S(1)} %fusion.88) | copy-start | bytes 393220
  291.8 109.7 %copy-start.6 = (bf16[128,1024]{1,0:T(8,128)(2,1)}, bf16[128,1024]{1,0:T(8,128)(2,1)S(1)}, u32[]{:S(2)}) copy-start(bf16[128,1024]{1,0:T(8,128)(2,1)S(1)} %multiply_convert_fusion.1) | copy-start | bytes 786436
  294.5 112.3 %copy-start.14 = (bf16[1,128,1024]{2,1,0:T(8,128)(2,1)S(1)}, bf16[1,128,1024]{2,1,0:T(8,128)(2,1)}, u32[]{:S(2)}) copy-start(bf16[1,128,1024]{2,1,0:T(8,128)(2,1)} %param.17) | copy-start | bytes 786436
  294.5 115.0 %all-to-all-start = ((bf16[32,48,1024]{2,1,0:T(8,128)(2,1)}), bf16[32,48,1024]{2,1,0:T(8,128)(2,1)}, u32[]{:S(2)}, u32[]{:S(2)}) async-start(bf16[32,48,1024]{2,1,0:T(8,128)(2,1)} %bitcast.24), calls=%async_computation | async-start | bytes 6291456 | tf_op jit(solution)/shard_map/all_to_all | solution.py:172
  299.1 152.8 %all-gather.29.cloned.1.call-start = ((), (), s32[]{:S(2)}) async-start(), calls=%async_computation.20 | async-start | bytes 5242880 | tf_op jit(solution)/shard_map/all_gather | solution.py:122
  409.5 75.1 %all-to-all-start.2 = ((bf16[32,48,1024]{2,1,0:T(8,128)(2,1)}), bf16[32,48,1024]{2,1,0:T(8,128)(2,1)S(1)}, u32[]{:S(2)}, u32[]{:S(2)}) async-start(bf16[32,48,1024]{2,1,0:T(8,128)(2,1)} %bitcast.43), calls=%async_computation.2 | async-start | bytes 6291456 | tf_op jit(solution)/shard_map/all_to_all | solution.py:226
  496.8 75.1 %all-to-all-start.1 = ((bf16[32,48,1024]{2,1,0:T(8,128)(2,1)}), bf16[32,48,1024]{2,1,0:T(8,128)(2,1)S(1)}, u32[]{:S(2)}, u32[]{:S(2)}) async-start(bf16[32,48,1024]{2,1,0:T(8,128)(2,1)} %bitcast.331), calls=%async_computation.1 | async-start | bytes 6291456 | tf_op jit(solution)/shard_map/all_to_all | solution.py:181
  571.9 92.8 %all-to-all-start.3 = ((bf16[32,48,1024]{2,1,0:T(8,128)(2,1)}), bf16[32,48,1024]{2,1,0:T(8,128)(2,1)}, u32[]{:S(2)}, u32[]{:S(2)}) async-start(bf16[32,48,1024]{2,1,0:T(8,128)(2,1)} %bitcast.330), calls=%async_computation.3 | async-start | bytes 6291456 | tf_op jit(solution)/shard_map/all_to_all | solution.py:255
  576.3 134.6 %all-gather.31.cloned.1.call-start = ((), (), s32[]{:S(2)}) async-start(), calls=%async_computation.21 | async-start | bytes 2359296 | tf_op jit(solution)/shard_map/all_gather | solution.py:311
  578.1 140.2 %all-gather.33.cloned.1.call-start = ((), (), s32[]{:S(2)}) async-start(), calls=%async_computation.22 | async-start | bytes 2359296 | tf_op jit(solution)/shard_map/all_gather | solution.py:312
  677.3 95.1 %reduce-scatter.23.cloned.1.call-start = ((), (), s32[]{:S(2)}) async-start(), calls=%async_computation.30 | async-start | bytes 5242880 | tf_op jit(solution)/shard_map/reduce_scatter | solution.py:269
  683.6 131.7 %reduce-scatter.19.cloned.1.call-start = ((), (), s32[]{:S(2)}) async-start(), calls=%async_computation.28 | async-start | bytes 5242880 | tf_op jit(solution)/shard_map/reduce_scatter | solution.py:263
  691.3 179.4 %reduce-scatter.21.cloned.1.call-start = ((), (), s32[]{:S(2)}) async-start(), calls=%async_computation.29 | async-start | bytes 5242880 | tf_op jit(solution)/shard_map/reduce_scatter | solution.py:266
  699.2 310.0 %reduce-scatter.17.cloned.1.call-start = ((), (), s32[]{:S(2)}) async-start(), calls=%async_computation.27 | async-start | bytes 540672 | tf_op jit(solution)/shard_map/reduce_scatter | solution.py:374
  718.2 428.9 %reduce-scatter.13.cloned.1.call-start = ((), (), s32[]{:S(2)}) async-start(), calls=%async_computation.25 | async-start | bytes 2162688 | tf_op jit(solution)/shard_map/reduce_scatter | solution.py:372
  730.4 554.7 %reduce-scatter.11.cloned.1.call-start = ((), (), s32[]{:S(2)}) async-start(), calls=%async_computation.24 | async-start | bytes 2162688 | tf_op jit(solution)/shard_map/reduce_scatter | solution.py:371
  754.9 673.8 %reduce-scatter.15.cloned.1.call-start = ((), (), s32[]{:S(2)}) async-start(), calls=%async_computation.26 | async-start | bytes 4325376 | tf_op jit(solution)/shard_map/reduce_scatter | solution.py:373
  757.8 814.0 %reduce-scatter.9.cloned.1.call-start = ((), (), s32[]{:S(2)}) async-start(), calls=%async_computation.23 | async-start | bytes 4325376 | tf_op jit(solution)/shard_map/reduce_scatter | solution.py:370
  775.3 98.4 %copy-start.9 = (bf16[1024,512]{1,0:T(8,128)(2,1)S(1)}, bf16[1024,512]{1,0:T(8,128)(2,1)}, u32[]{:S(2)}) copy-start(bf16[1024,512]{1,0:T(8,128)(2,1)} %all-gather.17.cloned.1.call-done) | copy-start | bytes 3145732
  775.3 98.4 %copy-start.21 = (f32[128,1024]{1,0:T(8,128)S(1)}, f32[128,1024]{1,0:T(8,128)}, u32[]{:S(2)}) copy-start(f32[128,1024]{1,0:T(8,128)} %fusion.142) | copy-start | bytes 1572868
  (72 other events, 908.0 us)
Sparse Core Ops, SparseCore 0:
  11.0 56.5 all-gather.12
  70.6 52.7 all-gather.16
  125.6 21.2 all-gather.14
  149.7 56.1 all-gather.20
  208.0 22.7 all-gather.18
  233.6 55.1 all-gather.22
  290.6 51.4 all-gather.24
  343.9 53.6 all-gather.26
  399.5 52.4 all-gather.28
  578.4 73.3 all-gather.30
  677.4 27.0 all-gather.32
  707.3 52.3 reduce-scatter.22
  762.7 52.5 reduce-scatter.18
  818.1 52.5 reduce-scatter.20
  873.4 135.7 reduce-scatter.16
  1011.9 135.1 reduce-scatter.12
  1149.8 135.2 reduce-scatter.10
  1287.8 140.8 reduce-scatter.14
  1431.6 140.1 reduce-scatter.8
where the time goes:
time: 1580 us
  waiting for transfers between devices  1130 us (72%)
  blocking collectives  213 us (13%)
  matrix products  109 us (7%)
  local copies, waits for them, and re-layouts  49 us (3%)
  other arithmetic  39.9 us (3%)
  starting transfers between devices  17.8 us (1%)
    reduce_scatter x1, waiting for transfers between devices, shards(): lax.psum_scatter(grad_w_output, ('batch', 'ctx'), scatter_dimension=0, ti...  144 us
    reduce_scatter x1, waiting for transfers between devices, shards(): lax.psum_scatter(grad_w_query, ('batch', 'ctx'), scatter_dimension=0, til...  143 us
    reduce_scatter x1, waiting for transfers between devices, shards(): lax.psum_scatter(grad_w_key, ('batch', 'ctx'), scatter_dimension=0, tiled...  138 us
    reduce_scatter x1, waiting for transfers between devices, shards(): lax.psum_scatter(grad_w_value, ('batch', 'ctx'), scatter_dimension=0, til...  138 us
    all_gather x1, blocking collectives, shards(): lax.all_gather(w_router, ('batch', 'ctx'), axis=0, tiled=True)  101 us
    reduce_scatter x1, waiting for transfers between devices, shards(): lax.psum_scatter(grad_router, ('batch', 'ctx'), scatter_dimension=0, tile...  92.9 us
    unnamed x2, blocking collectives  81.4 us
    all_to_all x1, waiting for transfers between devices, shards(): lax.all_to_all(grad_expert_in.reshape(EXPERTS, CAP, model_width), 'ctx',...  73.4 us
  transfers between devices with their start and end apart: 23, of which 16 were waited for; matrix products, arithmetic and copies ran while one was open for 11% of the time, Pallas kernels for 0%

commit v1 on v0

v1 whole, which is shorter than its diff:
```python
import math

import jax
import jax.numpy as jnp
from jax import lax
from jax.sharding import PartitionSpec as P

HEADS = 16
KV_HEADS = 8
HEAD_DIM = 64
CAP = 48


EPS = 1e-06
ROPE_BASE = 10000.0


def rope_tables(positions, head_size):
    half_size = head_size // 2
    exponent = jnp.arange(half_size, dtype=jnp.float32) * (2.0 / head_size)
    inverse = jnp.exp(-exponent * math.log(ROPE_BASE))
    angles = positions.astype(jnp.float32)[:, None] * inverse[None, :]
    return (jnp.cos(angles), jnp.sin(angles))


def rotate(values, cos_table, sin_table):
    half_size = values.shape[-1] // 2
    lower_half = values[..., :half_size]
    upper_half = values[..., half_size:]
    cos_part = cos_table[:, None, :]
    sin_part = sin_table[:, None, :]
    return jnp.concatenate(
        [
            lower_half * cos_part - upper_half * sin_part,
            upper_half * cos_part + lower_half * sin_part,
        ],
        axis=-1,
    )


def cdiv(value, step):
    return -(-value // step)


def exchange(blocks, axis, groups=None):
    return lax.all_to_all(
        blocks, axis, split_axis=0, concat_axis=0, axis_index_groups=groups, tiled=True
    )


def fold(blocks):
    return jnp.sum(blocks.astype(jnp.float32), axis=0).astype(jnp.bfloat16)


def scatter_sum(partial, batch_count, ctx_count):
    rows, columns = partial.shape
    own_rows = rows // (batch_count * ctx_count)
    pair = 2 if ctx_count % 2 == 0 else 1
    far = ctx_count // pair
    near_groups = [[f * pair + p for p in range(pair)] for f in range(far)]
    far_groups = [[f * pair + p for f in range(far)] for p in range(pair)]
    held = partial.reshape(batch_count, far, pair, own_rows, columns)
    held = jnp.transpose(held, (2, 0, 1, 3, 4))
    if pair > 1:
        held = exchange(held, "ctx", near_groups)
    held = fold(held)
    held = fold(exchange(held, "batch"))
    return jnp.sum(exchange(held, "ctx", far_groups).astype(jnp.float32), axis=0)


def attend(queries, key_rows, value_rows, allowed, score_scale):
    scores = (
        jnp.einsum("tkgd,skd->kgts", queries, key_rows, preferred_element_type=jnp.float32)
        * score_scale
    )
    exp_scores = jnp.where(allowed[None, None], jnp.exp(scores), 0.0)
    totals = jnp.sum(exp_scores, axis=-1, keepdims=True)
    prob_wire = (exp_scores / totals).astype(jnp.bfloat16)
    output = jnp.einsum("kgts,skd->tkgd", prob_wire, value_rows, preferred_element_type=jnp.float32)
    return (output.astype(jnp.bfloat16), jnp.log(totals))


def score_grads(
    queries, key_rows, value_rows, allowed, score_scale, log_totals, delta_heads, grad_rows
):
    scores = (
        jnp.einsum("tkgd,skd->kgts", queries, key_rows, preferred_element_type=jnp.float32)
        * score_scale
    )
    prob_again = jnp.where(allowed[None, None], jnp.exp(scores - log_totals), 0.0)
    grad_prob = jnp.einsum(
        "tkgd,skd->kgts", grad_rows, value_rows, preferred_element_type=jnp.float32
    )
    grad_score = (prob_again * (grad_prob - delta_heads) * score_scale).astype(jnp.bfloat16)
    return (prob_again.astype(jnp.bfloat16), grad_score)


def shards(
    inputs,
    segments,
    routes,
    cotangent,
    w_query,
    w_key,
    w_value,
    w_output,
    w_router,
    norm_attn,
    norm_moe,
    w_gate,
    w_up,
    w_down,
):
    tok_rows = inputs.shape[1]
    model_width = inputs.shape[2]
    ctx_count = lax.axis_size("ctx")
    batch_count = lax.axis_size("batch")
    ctx_index = lax.axis_index("ctx")
    batch_index = lax.axis_index("batch")
    device_count = ctx_count * batch_count
    seq_length = tok_rows * ctx_count
    groups_per = HEADS // KV_HEADS
    kv_width = KV_HEADS * HEAD_DIM
    query_width = HEADS * HEAD_DIM
    own_rows, experts = w_router.shape
    unit_count = w_gate.shape[2]
    held_experts = w_gate.shape[0]
    spread = held_experts % batch_count == 0
    slot_total = experts * CAP
    score_scale = 1.0 / math.sqrt(HEAD_DIM)
    residual_in = inputs[0].astype(jnp.float32)
    seg_local = segments[0]
    grad_wire = cotangent[0]
    grad_out = grad_wire.astype(jnp.float32)

    if spread:
        served = held_experts // batch_count
        token_axes = ("batch", "ctx")
        order = [
            (c * batch_count + b) * served + j
            for b in range(batch_count)
            for c in range(ctx_count)
            for j in range(served)
        ]
    else:
        served = held_experts
        token_axes = "ctx"
        order = list(range(experts))
    place = [order.index(e) for e in range(experts)]
    order_row = jnp.array(order, dtype=jnp.int32)
    route_mask = jnp.any(routes[0][:, :, None] == order_row[None, None, :], axis=1)
    token_row = jnp.arange(tok_rows, dtype=jnp.int32)
    before = (token_row[None, :] < token_row[:, None]).astype(jnp.bfloat16)
    turn = jnp.dot(
        before, route_mask.astype(jnp.bfloat16), preferred_element_type=jnp.float32
    ).astype(jnp.int32)
    slot_mask = route_mask[:, :, None] & (
        turn[:, :, None] == jnp.arange(CAP, dtype=jnp.int32)[None, None, :]
    )
    dispatch = slot_mask.astype(jnp.bfloat16).reshape(tok_rows, slot_total)

    def send_tokens(rows):
        picked = lax.dot_general(
            dispatch, rows, (((0,), (0,)), ((), ())), preferred_element_type=jnp.float32
        ).astype(jnp.bfloat16)
        arrived = exchange(picked.reshape(experts, CAP, model_width), token_axes)
        return arrived.reshape(-1, served, CAP, model_width)

    def return_tokens(rows):
        back = exchange(rows.reshape(experts, CAP, model_width), token_axes)
        return jnp.dot(
            dispatch, back.reshape(slot_total, model_width), preferred_element_type=jnp.float32
        )

    seg_columns = cdiv(tok_rows, own_rows)
    seg_pad = jnp.pad(seg_local, (0, seg_columns * own_rows - tok_rows))
    small_width = experts + 2 + seg_columns
    small_pad = cdiv(small_width, 128) * 128 - small_width
    dense_own = jnp.concatenate(
        [
            w_query,
            w_key,
            w_value,
            w_output,
            w_router[:, order_row] if spread else w_router,
            norm_attn[:, None],
            norm_moe[:, None],
            seg_pad.reshape(own_rows, seg_columns).astype(jnp.bfloat16),
            jnp.zeros((own_rows, small_pad), jnp.bfloat16),
        ],
        axis=1,
    )
    dense_full = lax.all_gather(dense_own, ("batch", "ctx"), axis=0, tiled=True)
    qkv_width = query_width + 2 * kv_width
    qkv_full = dense_full[:, :qkv_width]
    output_full = dense_full[:, qkv_width : qkv_width + model_width]
    small_full = dense_full[:, qkv_width + model_width :]
    router_full = small_full[:, :experts]
    gain_attn = small_full[:, experts].astype(jnp.float32)
    gain_moe = small_full[:, experts + 1].astype(jnp.float32)
    seg_devices = small_full[:, experts + 2 : small_width].reshape(batch_count, ctx_count, -1)
    seg_all = lax.dynamic_index_in_dim(
        seg_devices[:, :, :tok_rows].reshape(batch_count, seq_length),
        batch_index,
        0,
        keepdims=False,
    )

    expert_own = jnp.concatenate([w_gate, w_up, w_down], axis=2)
    if spread:
        expert_full = lax.all_to_all(
            expert_own, "batch", split_axis=0, concat_axis=1, tiled=True
        )
    else:
        expert_full = lax.all_gather(expert_own, "batch", axis=1, tiled=True)
    gate_up_full = expert_full[:, :, : 2 * unit_count]
    down_full = expert_full[:, :, 2 * unit_count :]
    grad_rows_moe = send_tokens(grad_wire)

    positions = ctx_index * tok_rows + jnp.arange(tok_rows, dtype=jnp.int32)
    cos_table, sin_table = rope_tables(positions, HEAD_DIM)
    inv_first = lax.rsqrt(jnp.mean(residual_in * residual_in, axis=-1, keepdims=True) + EPS)
    normed_attn = (residual_in * inv_first * gain_attn).astype(jnp.bfloat16)
    projected = jnp.dot(normed_attn, qkv_full, preferred_element_type=jnp.float32)
    rotated = rotate(
        projected[:, : query_width + kv_width].reshape(tok_rows, HEADS + KV_HEADS, HEAD_DIM),
        cos_table,
        sin_table,
    ).astype(jnp.bfloat16)
    query_rot = rotated[:, :HEADS]
    key_rot = rotated[:, HEADS:]
    value_rows = projected[:, query_width + kv_width :].astype(jnp.bfloat16)
    kv_all = lax.all_gather(
        jnp.concatenate([key_rot.reshape(tok_rows, kv_width), value_rows], axis=1),
        "ctx",
        axis=0,
        tiled=True,
    )
    seg_wire = seg_local.astype(jnp.bfloat16)
    key_pos = jnp.arange(seq_length, dtype=jnp.int32)
    allowed = (seg_wire[:, None] == seg_all[None, :]) & (key_pos[None, :] <= positions[:, None])
    query_groups = query_rot.reshape(tok_rows, KV_HEADS, groups_per, HEAD_DIM)
    key_heads = kv_all[:, :kv_width].reshape(seq_length, KV_HEADS, HEAD_DIM)
    value_heads = kv_all[:, kv_width:].reshape(seq_length, KV_HEADS, HEAD_DIM)
    attn_rows, log_totals = attend(query_groups, key_heads, value_heads, allowed, score_scale)
    attn_flat = attn_rows.reshape(tok_rows, query_width)
    hidden_res = residual_in + jnp.dot(attn_flat, output_full, preferred_element_type=jnp.float32)
    inv_second = lax.rsqrt(jnp.mean(hidden_res * hidden_res, axis=-1, keepdims=True) + EPS)
    normed_moe = (hidden_res * inv_second * gain_moe).astype(jnp.bfloat16)

    logits = jnp.dot(normed_moe, router_full, preferred_element_type=jnp.float32)
    route_exp = jnp.where(route_mask, jnp.exp(logits), 0.0)
    route_weights = route_exp / jnp.sum(route_exp, axis=-1, keepdims=True)
    slot_weight = jnp.sum(jnp.where(slot_mask, route_weights[:, :, None], 0.0), axis=0)
    arrived = send_tokens(normed_moe)
    weight_arrived = exchange(slot_weight, token_axes).reshape(-1, served, CAP)[..., None]

    gate_up = jnp.einsum("gesd,edf->gesf", arrived, gate_up_full, preferred_element_type=jnp.float32)
    gate_pre = gate_up[..., :unit_count]
    up_pre = gate_up[..., unit_count:]
    sigmoid_gate = jax.nn.sigmoid(gate_pre)
    silu_gate = gate_pre * sigmoid_gate
    hidden_act = (silu_gate * up_pre).astype(jnp.bfloat16)
    expert_out = jnp.einsum(
        "gesf,edf->gesd", hidden_act, down_full, preferred_element_type=jnp.float32
    )
    grad_rows_wide = grad_rows_moe.astype(jnp.float32)
    grad_dots = jnp.sum(grad_rows_wide * expert_out, axis=-1)
    dots_back = exchange(grad_dots.reshape(experts, CAP), token_axes)
    grad_slots = (weight_arrived * grad_rows_wide).astype(jnp.bfloat16)
    grad_hidden = jnp.einsum(
        "gesd,edf->gesf", grad_slots, down_full, preferred_element_type=jnp.float32
    )
    grad_gate = grad_hidden * up_pre * sigmoid_gate * (1.0 + gate_pre * (1.0 - sigmoid_gate))
    grad_up = grad_hidden * silu_gate
    grad_gate_up = jnp.concatenate([grad_gate, grad_up], axis=-1).astype(jnp.bfloat16)
    grad_expert_in = jnp.einsum(
        "gesf,edf->gesd", grad_gate_up, gate_up_full, preferred_element_type=jnp.float32
    ).astype(jnp.bfloat16)
    grad_from_experts = return_tokens(grad_expert_in)
    grad_w_gate_up = jnp.einsum(
        "gesd,gesf->edf", arrived, grad_gate_up, preferred_element_type=jnp.float32
    )
    grad_w_down = jnp.einsum(
        "gesd,gesf->edf", grad_slots, hidden_act, preferred_element_type=jnp.float32
    )
    grad_experts = jnp.concatenate([grad_w_gate_up, grad_w_down], axis=2).astype(jnp.bfloat16)
    weighted_out = (weight_arrived * expert_out).astype(jnp.bfloat16)
    if spread:
        expert_sum = lax.all_to_all(
            grad_experts, "batch", split_axis=1, concat_axis=0, tiled=True
        )
    else:
        expert_sum = lax.psum_scatter(grad_experts, "batch", scatter_dimension=1, tiled=True)
    expert_sum = expert_sum.astype(jnp.float32)
    moe_out = return_tokens(weighted_out)
    block_out = (hidden_res + moe_out).astype(jnp.bfloat16)

    grad_weights = jnp.sum(jnp.where(slot_mask, dots_back[None], 0.0), axis=-1)
    grad_chosen = route_weights * (
        grad_weights - jnp.sum(route_weights * grad_weights, axis=-1, keepdims=True)
    )
    grad_logits = grad_chosen.astype(jnp.bfloat16)
    grad_router = jnp.dot(normed_moe.T, grad_logits, preferred_element_type=jnp.float32)
    grad_normed = (
        jnp.dot(grad_logits, router_full.T, preferred_element_type=jnp.float32)
        + grad_from_experts
    )
    gained_moe = grad_normed * gain_moe
    grad_gain_moe = jnp.sum(grad_normed * hidden_res * inv_second, axis=0)
    grad_hidden_res = (
        grad_out
        + inv_second * gained_moe
        - hidden_res * inv_second**3 * jnp.mean(gained_moe * hidden_res, axis=-1, keepdims=True)
    )
    grad_attn = grad_hidden_res.astype(jnp.bfloat16)
    grad_w_output = jnp.dot(attn_flat.T, grad_attn, preferred_element_type=jnp.float32)
    tail_pad = cdiv(experts + 1, 128) * 128 - experts - 1
    first_sum = scatter_sum(
        jnp.concatenate(
            [
                grad_w_output,
                grad_router,
                grad_gain_moe[:, None],
                jnp.zeros((model_width, tail_pad), jnp.float32),
            ],
            axis=1,
        ).astype(jnp.bfloat16),
        batch_count,
        ctx_count,
    )

    grad_attn_rows = (
        jnp.dot(grad_attn, output_full.T, preferred_element_type=jnp.float32)
        .astype(jnp.bfloat16)
        .reshape(tok_rows, KV_HEADS, groups_per, HEAD_DIM)
    )
    delta_rows = jnp.sum(
        grad_attn_rows.astype(jnp.float32) * attn_rows.astype(jnp.float32), axis=-1
    )
    query_all = lax.all_gather(query_rot.reshape(tok_rows, query_width), "ctx", axis=0, tiled=True)
    grad_rows_all = lax.all_gather(
        grad_attn_rows.reshape(tok_rows, query_width), "ctx", axis=0, tiled=True
    )
    stats_all = lax.all_gather(
        jnp.concatenate(
            [
                jnp.transpose(log_totals[..., 0], (2, 0, 1)).reshape(tok_rows, HEADS),
                delta_rows.reshape(tok_rows, HEADS),
            ],
            axis=1,
        ),
        "ctx",
        axis=0,
        tiled=True,
    )
    prob_wire, grad_score = score_grads(
        query_groups,
        key_heads,
        value_heads,
        allowed,
        score_scale,
        log_totals,
        jnp.transpose(delta_rows, (1, 2, 0))[..., None],
        grad_attn_rows,
    )
    grad_query_rot = jnp.einsum(
        "kgts,skd->tkgd", grad_score, key_heads, preferred_element_type=jnp.float32
    )
    log_all = stats_all[:, :HEADS].reshape(seq_length, KV_HEADS, groups_per)
    delta_all = stats_all[:, HEADS:].reshape(seq_length, KV_HEADS, groups_per)
    query_seq = query_all.reshape(seq_length, KV_HEADS, groups_per, HEAD_DIM)
    grad_seq = grad_rows_all.reshape(seq_length, KV_HEADS, groups_per, HEAD_DIM)
    allowed_keys = (seg_all[:, None] == seg_wire[None, :]) & (
        positions[None, :] <= key_pos[:, None]
    )
    prob_keys, score_keys = score_grads(
        query_seq,
        key_rot,
        value_rows.reshape(tok_rows, KV_HEADS, HEAD_DIM),
        allowed_keys,
        score_scale,
        jnp.transpose(log_all, (1, 2, 0))[..., None],
        jnp.transpose(delta_all, (1, 2, 0))[..., None],
        grad_seq,
    )
    grad_key_own = jnp.einsum(
        "kgts,tkgd->skd", score_keys, query_seq, preferred_element_type=jnp.float32
    )
    grad_value_own = jnp.einsum(
        "kgts,tkgd->skd", prob_keys, grad_seq, preferred_element_type=jnp.float32
    )
    grad_rotated = rotate(
        jnp.concatenate(
            [grad_query_rot.reshape(tok_rows, HEADS, HEAD_DIM), grad_key_own], axis=1
        ),
        cos_table,
        -sin_table,
    )
    grad_qkv = jnp.concatenate(
        [
            grad_rotated.reshape(tok_rows, query_width + kv_width),
            grad_value_own.reshape(tok_rows, kv_width),
        ],
        axis=1,
    ).astype(jnp.bfloat16)
    grad_w_qkv = jnp.dot(normed_attn.T, grad_qkv, preferred_element_type=jnp.float32)
    grad_normed_attn = jnp.dot(grad_qkv, qkv_full.T, preferred_element_type=jnp.float32)
    gained_attn = grad_normed_attn * gain_attn
    grad_gain_attn = jnp.sum(grad_normed_attn * residual_in * inv_first, axis=0)
    grad_inputs = (
        grad_hidden_res
        + inv_first * gained_attn
        - residual_in * inv_first**3 * jnp.mean(gained_attn * residual_in, axis=-1, keepdims=True)
    )
    last_sum = scatter_sum(
        jnp.concatenate(
            [
                grad_w_qkv,
                grad_gain_attn[:, None],
                jnp.zeros((model_width, 127), jnp.float32),
            ],
            axis=1,
        ).astype(jnp.bfloat16),
        batch_count,
        ctx_count,
    )
    router_sum = first_sum[:, model_width : model_width + experts]
    if spread:
        router_sum = router_sum[:, jnp.array(place, dtype=jnp.int32)]
    return (
        block_out[None],
        grad_inputs[None],
        last_sum[:, :query_width],
        last_sum[:, query_width : query_width + kv_width],
        last_sum[:, query_width + kv_width : qkv_width],
        first_sum[:, :model_width],
        router_sum,
        last_sum[:, qkv_width],
        first_sum[:, model_width + experts],
        expert_sum[:, :, :unit_count],
        expert_sum[:, :, unit_count : 2 * unit_count],
        expert_sum[:, :, 2 * unit_count :],
    )


def solution(mesh):
    placed = (
        P("batch", "ctx", None),
        P("batch", "ctx"),
        P("batch", "ctx", None),
        P("batch", "ctx", None),
        P(("batch", "ctx"), None),
        P(("batch", "ctx"), None),
        P(("batch", "ctx"), None),
        P(("batch", "ctx"), None),
        P(("batch", "ctx"), None),
        P(("batch", "ctx")),
        P(("batch", "ctx")),
        P("ctx", "batch", None),
        P("ctx", "batch", None),
        P("ctx", "batch", None),
    )
    return jax.shard_map(
        shards,
        mesh=mesh,
        in_specs=placed,
        out_specs=(
            P("batch", "ctx", None),
            P("batch", "ctx", None),
            P(("batch", "ctx"), None),
            P(("batch", "ctx"), None),
            P(("batch", "ctx"), None),
            P(("batch", "ctx"), None),
            P(("batch", "ctx"), None),
            P(("batch", "ctx")),
            P(("batch", "ctx")),
            P("ctx", "batch", None),
            P("ctx", "batch", None),
            P("ctx", "batch", None),
        ),
        check_vma=False,
    )
```

time: 1580 us -> 727 us (0.46)
  waiting for transfers between devices: 1130 us -> 312 us
  blocking collectives: 213 us -> 91.2 us
  local copies, waits for them, and re-layouts: 49 us -> 95.3 us
  starting transfers between devices: 17.8 us -> 43.3 us
  other arithmetic: 39.9 us -> 59.7 us
    reduce_scatter x8 -> x0, waiting for transfers between devices: 748 us -> none  [the longest x1 144 us: shards(): lax.psum_scatter(grad_w_output, ('batch', 'ctx'), scatter_dimension=0, ti...]
    all_gather x9 -> x2, waiting for transfers between devices: 212 us -> 84.7 us  [the longest x1 70.8 us: shards(): dense_full = lax.all_gather(dense_own, ('batch', 'ctx'), axis=0, tiled=True)]
    unnamed x2 -> x0, blocking collectives: 81.4 us -> none
    all_gather x4 -> x1, blocking collectives: 132 us -> 63 us  [shards(): lax.all_gather(jnp.concatenate([jnp.transpose(log_totals[..., 0], (2, 0,...]
    all_to_all x4 -> x11, waiting for transfers between devices: 169 us -> 227 us  [the longest x9 213 us: exchange(): lax.all_to_all(blocks, axis, split_axis=0, concat_axis=0, axis_index_grou...]
    all_to_all x0 -> x3, blocking collectives: none -> 28.1 us  [exchange(): lax.all_to_all(blocks, axis, split_axis=0, concat_axis=0, axis_index_grou...]
    concatenate x0 -> x6, local copies, waits for them, and re-layouts: none -> 26.5 us  [the longest x1 11.6 us: shards(): jnp.concatenate([grad_w_gate_up, grad_w_down], axis=2).astype(jnp.bfloat16)]
    all_to_all x4 -> x11, starting transfers between devices: 16.4 us -> 42.7 us  [the longest x9 34.2 us: exchange(): lax.all_to_all(blocks, axis, split_axis=0, concat_axis=0, axis_index_grou...]
  transfers between devices with their start and end apart: 23 -> 15, of which waited for: 16 -> 10; matrix products, arithmetic and copies ran while one was open for 11% -> 30% of each run, Pallas kernels for 0% -> 0%
where the time goes in v1:
time: 727 us; the launch traced here: 716 us
  waiting for transfers between devices  312 us (43%)
  matrix products  100 us (14%)
  local copies, waits for them, and re-layouts  95.3 us (13%)
  blocking collectives  91.2 us (13%)
  other arithmetic  59.7 us (8%)
  starting transfers between devices  43.3 us (6%)
  between operations  14.9 us (2%)
    all_to_all x9, waiting for transfers between devices, exchange(): lax.all_to_all(blocks, axis, split_axis=0, concat_axis=0, axis_index_grou...  213 us
    all_gather x1, waiting for transfers between devices, shards(): dense_full = lax.all_gather(dense_own, ('batch', 'ctx'), axis=0, tiled=True)  70.8 us
    all_gather x1, blocking collectives, shards(): lax.all_gather(jnp.concatenate([jnp.transpose(log_totals[..., 0], (2, 0,...  63 us
    all_to_all x9, starting transfers between devices, exchange(): lax.all_to_all(blocks, axis, split_axis=0, concat_axis=0, axis_index_grou...  34.2 us
    all_to_all x3, blocking collectives, exchange(): lax.all_to_all(blocks, axis, split_axis=0, concat_axis=0, axis_index_grou...  28.1 us
    unnamed x119, local copies, waits for them, and re-layouts  26.9 us
    unnamed x1, other arithmetic  20.3 us
  transfers between devices with their start and end apart: 15, of which 10 were waited for; matrix products, arithmetic and copies ran while one was open for 30% of the time, Pallas kernels for 0%

profile of v1, /device:TPU:0, one launch (start us, length us, event | category | flops | bytes accessed | tf_op | source)
XLA Modules:
  0.0 716.4 jit_solution(12469723728471024564)
XLA Ops:
  15.8 70.8 %all-gather.5.cloned.1.call-done = bf16[1024,3200]{1,0:T(8,128)(2,1)} async-done(((bf16[32,3200]{1,0:T(8,128)(2,1)}), bf16[1024,3200]{1,0:T(8,128)(2,1)}) %all-gather.5.cloned.1.call-update) | async-done | bytes 6553616 | tf_op jit(solution)/shard_map/all_gather | solution.py:193
  106.9 14.0 %all-gather.7.cloned.1.call-done = bf16[1024,1024]{1,0:T(8,128)(2,1)} async-done(((bf16[128,1024]{1,0:T(8,128)(2,1)}), bf16[1024,1024]{1,0:T(8,128)(2,1)}) %all-gather.7.cloned.1.call-update) | async-done | bytes 2097168 | tf_op jit(solution)/shard_map/all_gather | solution.py:233
  151.6 68.1 %all-to-all-done.2 = bf16[32,48,1024]{2,1,0:T(8,128)(2,1)} async-done(((bf16[32,48,1024]{2,1,0:T(8,128)(2,1)}), bf16[32,48,1024]{2,1,0:T(8,128)(2,1)}, u32[]{:S(2)}, u32[]{:S(2)}) %all-to-all-start.2) | async-done | bytes 3145760 | tf_op jit(solution)/shard_map/all_to_all | solution.py:46
  225.0 6.0 convolution_bitcast_fusion
  235.9 59.3 %all-to-all-done.4 = bf16[32,48,1024]{2,1,0:T(8,128)(2,1)S(1)} async-done(((bf16[32,48,1024]{2,1,0:T(8,128)(2,1)}), bf16[32,48,1024]{2,1,0:T(8,128)(2,1)S(1)}, u32[]{:S(2)}, u32[]{:S(2)}) %all-to-all-start.4) | async-done | bytes 3145760 | tf_op jit(solution)/shard_map/all_to_all | solution.py:46
  295.2 6.9 fusion.14
  304.7 7.1 all-to-all-done.5
  312.3 8.9 %all_to_all.89 = f32[32,1,48]{2,1,0:T(1,128)S(1)} all-to-all(f32[32,1,48]{2,1,0:T(1,128)S(1)} %bitcast.334), channel_id=1, replica_groups=mesh['batch'=4,'ctx'=8] {'batch','ctx'}, dimensions={0} | all-to-all | bytes 12288 | tf_op jit(solution)/shard_map/all_to_all | solution.py:46
  321.2 5.4 fusion.54
  328.3 4.9 convert_bitcast_fusion.1
  341.0 5.7 fusion.49
  347.1 11.6 %copy.158 = bf16[1,1024,1536]{2,0,1:T(2,128)(2,1)} copy(bf16[1,1024,1536]{1,2,0:T(8,128)(2,1)S(1)} %pad_maximum_fusion.2) | data formatting | bytes 6291456 | tf_op jit(solution)/shard_map/concatenate | solution.py:287
  359.2 20.3 %reduce.19 = bf16[1024,1536]{1,0:T(8,128)(2,1)S(1)} reduce(bf16[1024,1,1536]{2,1,0:T(2,128)(2,1)} %bitcast.295, bf16[]{:T(256)} %broadcast.319), dimensions={1}, to_apply=%bitcast.260.reduce_sub_computation | reduce | bytes 6291458
  383.1 43.0 %all-to-all-done.6 = bf16[32,48,1024]{2,1,0:T(8,128)(2,1)} async-done(((bf16[32,48,1024]{2,1,0:T(8,128)(2,1)}), bf16[32,48,1024]{2,1,0:T(8,128)(2,1)}, u32[]{:S(2)}, u32[]{:S(2)}) %all-to-all-start.6) | async-done | bytes 3145760 | tf_op jit(solution)/shard_map/all_to_all | solution.py:46
  439.3 4.9 fusion.35
  453.8 13.3 %all-to-all-done.13 = bf16[4,2,196608]{2,1,0:T(2,128)(2,1)} async-done(((bf16[4,2,196608]{2,1,0:T(2,128)(2,1)}), bf16[4,2,196608]{2,1,0:T(2,128)(2,1)}, u32[]{:S(2)}, u32[]{:S(2)}) %all-to-all-start.13) | async-done | bytes 3145760 | tf_op jit(solution)/shard_map/all_to_all | solution.py:290
  467.1 6.8 all_to_all.90
  482.2 6.1 fusion.98
  491.9 63.0 %all_gather.18 = f32[1024,32]{0,1:T(8,128)S(1)} all-gather(f32[128,32]{0,1:T(8,128)S(1)} %pad_maximum_fusion.15), channel_id=1, replica_groups=mesh['batch'=4,'ctx'=8] {'ctx'}, dimensions={0}, use_global_device_ids=true | all-gather | bytes 147456 | tf_op jit(solution)/shard_map/all_gather | solution.py:345
  558.0 8.1 %fusion.21 = f32[8,64,2,128]{3,1,2,0:T(8,128)} fusion(bf16[1024,8,64,1]{0,2,3,1:T(8,128)(2,1)} %bitcast.318, f32[8,1024,128,2]{2,1,3,0:T(8,128)} %copy-done.51, f32[8,2,128]{2,1,0:T(2,128)} %bitcast.336, f32[8,2,128]{2,1,0:T(2,128)} %log.13, pred[128,1024]{0,1:T(8,128)(4,1)S(1)} %copy-done.26, bf16[1024,8,64,1]{0,2,3,1:T(8,128)(2,1)} %bitcast.315, ...), kind=kOutput, calls=%fused_computation.31 | convolution fusion | flops 551550976 | bytes 11419648 | tf_op jit(solution)/shard_map/kgts,skd->tkgd/dot_general | solution.py:367
  570.1 5.8 fusion.74
  576.1 9.0 %fusion.68 = f32[128,8,64]{0,2,1:T(8,128)} fusion(bf16[1024,8,2,64]{0,3,2,1:T(8,128)(2,1)S(1)} %bitcast.301, f32[8,128,1024,2]{2,1,3,0:T(8,128)} %fusion.98, f32[8,2,1024]{2,1,0:T(2,128)} %bitcast.332, f32[8,2,1024]{2,1,0:T(2,128)} %bitcast.330, pred[1024,128]{0,1:T(8,128)(4,1)} %fusion.92, bf16[128,8,64,1]{0,2,3,1:T(8,128)(2,1)} %bitcast.324, ...), kind=kOutput, calls=%fused_computation.88 | convolution fusion | flops 551550976 | bytes 13238272 | tf_op jit(solution)/shard_map/kgts,tkgd->skd/dot_general | solution.py:387
  595.7 7.8 %concatenate.83 = bf16[4,4,2,32,2176]{4,3,2,1,0:T(8,128)(2,1)} concatenate(bf16[4,4,2,32,2048]{4,3,2,1,0:T(8,128)(2,1)} %convolution_convert_fusion.2, bf16[4,4,2,32,1]{4,3,2,1,0:T(8,128)(2,1)S(1)} %concatenate.90, bf16[4,4,2,32,127]{4,3,2,1,0:T(8,128)(2,1)S(1)} %broadcast_in_dim.139), dimensions={4} | concatenate | bytes 8912896 | tf_op jit(solution)/shard_map/concatenate | solution.py:417
  608.2 12.4 %all_to_all.91 = bf16[2,4,4,32,2176]{4,3,2,1,0:T(8,128)(2,1)} all-to-all(bf16[2,4,4,32,2176]{4,3,2,1,0:T(8,128)(2,1)} %copy.153), channel_id=1, replica_groups={{0,1},{2,3},{4,5},{6,7},{8,9},{10,11},{12,13},{14,15},{16,17},{18,19},{..., dimensions={0} | all-to-all | bytes 8912896 | tf_op jit(solution)/shard_map/all_to_all | solution.py:46
  624.5 5.1 reduce_sum.195
  629.6 10.3 %all-to-all-done.11 = bf16[4,4,32,1152]{3,2,1,0:T(8,128)(2,1)S(1)} async-done(((bf16[4,4,32,1152]{3,2,1,0:T(8,128)(2,1)}), bf16[4,4,32,1152]{3,2,1,0:T(8,128)(2,1)S(1)}, u32[]{:S(2)}, u32[]{:S(2)}) %all-to-all-start.11) | async-done | bytes 1179680 | tf_op jit(solution)/shard_map/all_to_all | solution.py:46
  646.7 23.5 %all-to-all-done.8 = bf16[4,4,32,2176]{3,2,1,0:T(8,128)(2,1)S(1)} async-done(((bf16[4,4,32,2176]{3,2,1,0:T(8,128)(2,1)}), bf16[4,4,32,2176]{3,2,1,0:T(8,128)(2,1)S(1)}, u32[]{:S(2)}, u32[]{:S(2)}) %all-to-all-start.8) | async-done | bytes 2228256 | tf_op jit(solution)/shard_map/all_to_all | solution.py:46
  670.2 4.8 all-to-all-start.12
  675.1 6.2 reshape.593
  681.3 6.0 copy.172
  688.6 5.1 all-to-all-start.9
  693.7 5.7 fusion.120
  (243 shorter events, 165.6 us)
Async XLA Ops:
  7.2 79.4 %all-gather.5.cloned.1.call-start = ((), (), s32[]{:S(2)}) async-start(), calls=%async_computation.14 | async-start | bytes 6758400 | tf_op jit(solution)/shard_map/all_gather | solution.py:193
  13.4 107.6 %all-gather.7.cloned.1.call-start = ((), (), s32[]{:S(2)}) async-start(), calls=%async_computation.15 | async-start | bytes 2359296 | tf_op jit(solution)/shard_map/all_gather | solution.py:233
  15.1 76.6 %copy-start.46 = (f32[128]{0:T(128)}, f32[128]{0:T(128)S(1)}, u32[]{:S(2)}) copy-start(f32[128]{0:T(128)S(1)} %get-tuple-element.101) | copy-start | bytes 1540
  15.8 76.2 %copy-start.24 = (f32[128,32]{0,1:T(8,128)}, f32[128,32]{0,1:T(8,128)S(1)}, u32[]{:S(2)}) copy-start(f32[128,32]{0,1:T(8,128)S(1)} %get-tuple-element.99) | copy-start | bytes 49156
  96.1 45.3 %all-to-all-start.1 = ((bf16[4,256,1536]{2,1,0:T(8,128)(2,1)}), bf16[4,256,1536]{2,1,0:T(8,128)(2,1)S(1)}, u32[]{:S(2)}, u32[]{:S(2)}) async-start(bf16[4,256,1536]{2,1,0:T(8,128)(2,1)} %pad_maximum_fusion), calls=%async_computation.1 | async-start | bytes 6291456 | tf_op jit(solution)/shard_map/all_to_all | solution.py:211
  100.2 20.7 %copy-start.21 = (pred[128,32]{0,1:T(8,128)(4,1)}, pred[128,32]{0,1:T(8,128)(4,1)S(1)}, u32[]{:S(2)}) copy-start(pred[128,32]{0,1:T(8,128)(4,1)S(1)} %compare_reduce_fusion) | copy-start | bytes 12292
  101.3 19.6 %copy-start.42 = (s32[128]{0:T(128)}, s32[128]{0:T(128)S(1)}, u32[]{:S(2)}) copy-start(s32[128]{0:T(128)S(1)} %iota_add_fusion) | copy-start | bytes 1540
  101.3 19.6 %copy-start.43 = (bf16[128]{0:T(256)(128)(2,1)}, bf16[128]{0:T(256)(128)(2,1)S(1)}, u32[]{:S(2)}) copy-start(bf16[128]{0:T(256)(128)(2,1)S(1)} %convert_bitcast_fusion.2) | copy-start | bytes 772
  104.4 16.5 %copy-start.34 = (bf16[1024]{0:T(1024)(128)(2,1)}, bf16[1024]{0:T(1024)(128)(2,1)S(1)}, u32[]{:S(2)}) copy-start(bf16[1024]{0:T(1024)(128)(2,1)S(1)} %dynamic-slice_reduce_fusion) | copy-start | bytes 6148
  138.7 83.9 %copy-start.7 = (bf16[128,1024]{1,0:T(8,128)(2,1)}, bf16[128,1024]{1,0:T(8,128)(2,1)S(1)}, u32[]{:S(2)}) copy-start(bf16[128,1024]{1,0:T(8,128)(2,1)S(1)} %multiply_convert_fusion.1) | copy-start | bytes 786436
  143.1 76.6 %all-to-all-start.2 = ((bf16[32,48,1024]{2,1,0:T(8,128)(2,1)}), bf16[32,48,1024]{2,1,0:T(8,128)(2,1)}, u32[]{:S(2)}, u32[]{:S(2)}) async-start(bf16[32,48,1024]{2,1,0:T(8,128)(2,1)} %bitcast.28), calls=%async_computation.2 | async-start | bytes 6291456 | tf_op jit(solution)/shard_map/all_to_all | solution.py:46
  219.7 75.5 %all-to-all-start.4 = ((bf16[32,48,1024]{2,1,0:T(8,128)(2,1)}), bf16[32,48,1024]{2,1,0:T(8,128)(2,1)S(1)}, u32[]{:S(2)}, u32[]{:S(2)}) async-start(bf16[32,48,1024]{2,1,0:T(8,128)(2,1)} %bitcast.298), calls=%async_computation.4 | async-start | bytes 6291456 | tf_op jit(solution)/shard_map/all_to_all | solution.py:46
  235.9 68.7 %copy-start.20 = (f32[128,32]{0,1:T(8,128)S(1)}, f32[128,32]{0,1:T(8,128)}, u32[]{:S(2)}) copy-start(f32[128,32]{0,1:T(8,128)} %get-tuple-element.111) | copy-start | bytes 49156
  235.9 68.8 %copy-start.37 = (f32[128]{0:T(128)S(1)}, f32[128]{0:T(128)}, u32[]{:S(2)}) copy-start(f32[128]{0:T(128)} %get-tuple-element.110) | copy-start | bytes 1540
  235.9 75.8 %copy-start.22 = (pred[128,32]{0,1:T(8,128)(4,1)S(1)}, pred[128,32]{0,1:T(8,128)(4,1)}, u32[]{:S(2)}) copy-start(pred[128,32]{0,1:T(8,128)(4,1)} %copy-done.21) | copy-start | bytes 12292
  302.1 9.6 %all-to-all-start.5 = ((f32[32,1,48]{2,1,0:T(1,128)}), f32[32,1,48]{2,1,0:T(1,128)S(1)}, u32[]{:S(2)}, u32[]{:S(2)}) async-start(f32[32,1,48]{2,1,0:T(1,128)} %bitcast.43), calls=%async_computation.5 | async-start | bytes 32768 | tf_op jit(solution)/shard_map/all_to_all | solution.py:46
  321.2 16.3 %copy-start.30 = (f32[32,1,48]{2,1,0:T(1,128)}, f32[32,1,48]{2,1,0:T(1,128)S(1)}, u32[]{:S(2)}) copy-start(f32[32,1,48]{2,1,0:T(1,128)S(1)} %all_to_all.89) | copy-start | bytes 18436
  321.2 7.1 copy-start.5
  333.2 92.9 %all-to-all-start.6 = ((bf16[32,48,1024]{2,1,0:T(8,128)(2,1)}), bf16[32,48,1024]{2,1,0:T(8,128)(2,1)}, u32[]{:S(2)}, u32[]{:S(2)}) async-start(bf16[32,48,1024]{2,1,0:T(8,128)(2,1)} %convert_bitcast_fusion.1), calls=%async_computation.6 | async-start | bytes 6291456 | tf_op jit(solution)/shard_map/all_to_all | solution.py:46
  336.7 145.5 %all-gather.9.cloned.1.call-start = ((), (), s32[]{:S(2)}) async-start(), calls=%async_computation.16 | async-start | bytes 2359296 | tf_op jit(solution)/shard_map/all_gather | solution.py:341
  426.1 41.0 %all-to-all-start.13 = ((bf16[4,2,196608]{2,1,0:T(2,128)(2,1)}), bf16[4,2,196608]{2,1,0:T(2,128)(2,1)}, u32[]{:S(2)}, u32[]{:S(2)}) async-start(bf16[4,2,196608]{2,1,0:T(2,128)(2,1)} %reshape.592), calls=%async_computation.13 | async-start | bytes 6291456 | tf_op jit(solution)/shard_map/all_to_all | solution.py:290
  430.8 135.3 %all-gather.11.cloned.1.call-start = ((), (), s32[]{:S(2)}) async-start(), calls=%async_computation.17 | async-start | bytes 2359296 | tf_op jit(solution)/shard_map/all_gather | solution.py:342
  439.3 6.0 copy-start.12
  473.9 134.3 %all-to-all-start.3 = ((bf16[32,48,1024]{2,1,0:T(8,128)(2,1)}), bf16[32,48,1024]{2,1,0:T(8,128)(2,1)}, u32[]{:S(2)}, u32[]{:S(2)}) async-start(bf16[32,48,1024]{2,1,0:T(8,128)(2,1)} %fusion.35), calls=%async_computation.3 | async-start | bytes 6291456 | tf_op jit(solution)/shard_map/all_to_all | solution.py:46
  570.1 6.0 copy-start.2
  576.1 10.7 %copy-start.10 = (bf16[1,128,1024]{2,1,0:T(8,128)(2,1)S(1)}, bf16[1,128,1024]{2,1,0:T(8,128)(2,1)}, u32[]{:S(2)}) copy-start(bf16[1,128,1024]{2,1,0:T(8,128)(2,1)} %param.16) | copy-start | bytes 786436
  620.6 19.2 %all-to-all-start.11 = ((bf16[4,4,32,1152]{3,2,1,0:T(8,128)(2,1)}), bf16[4,4,32,1152]{3,2,1,0:T(8,128)(2,1)S(1)}, u32[]{:S(2)}, u32[]{:S(2)}) async-start(bf16[4,4,32,1152]{3,2,1,0:T(8,128)(2,1)} %reduce_sum.199), calls=%async_computation.11 | async-start | bytes 2359296 | tf_op jit(solution)/shard_map/all_to_all | solution.py:46
  629.6 45.5 %copy-start.48 = (s32[32]{0:T(128)S(1)}, s32[32]{0:T(128)}, u32[]{:S(2)}) copy-start(s32[32]{0:T(128)} %constant.72) | copy-start | bytes 388
  640.9 29.4 %all-to-all-start.8 = ((bf16[4,4,32,2176]{3,2,1,0:T(8,128)(2,1)}), bf16[4,4,32,2176]{3,2,1,0:T(8,128)(2,1)S(1)}, u32[]{:S(2)}, u32[]{:S(2)}) async-start(bf16[4,4,32,2176]{3,2,1,0:T(8,128)(2,1)} %reduce_sum.195), calls=%async_computation.8 | async-start | bytes 4456448 | tf_op jit(solution)/shard_map/all_to_all | solution.py:46
  670.2 18.4 %all-to-all-start.12 = ((bf16[4,32,1152]{2,1,0:T(8,128)(2,1)}), bf16[4,32,1152]{2,1,0:T(8,128)(2,1)S(1)}, u32[]{:S(2)}, u32[]{:S(2)}) async-start(bf16[4,32,1152]{2,1,0:T(8,128)(2,1)} %reduce_sum.200), calls=%async_computation.12 | async-start | bytes 589824 | tf_op jit(solution)/shard_map/all_to_all | solution.py:46
  688.6 19.0 %all-to-all-start.9 = ((bf16[4,32,2176]{2,1,0:T(8,128)(2,1)}), bf16[4,32,2176]{2,1,0:T(8,128)(2,1)S(1)}, u32[]{:S(2)}, u32[]{:S(2)}) async-start(bf16[4,32,2176]{2,1,0:T(8,128)(2,1)} %reduce_sum.196), calls=%async_computation.9 | async-start | bytes 1114112 | tf_op jit(solution)/shard_map/all_to_all | solution.py:46
  693.7 5.7 copy-start.23
  (39 other events, 120.5 us)
Sparse Core Ops, SparseCore 0:
  13.5 73.0 all-gather.4
  93.2 27.6 all-gather.6
  339.1 59.5 all-gather.8
  438.4 27.7 all-gather.10

commit v2 on v1

--- a/solution.py
+++ b/solution.py
@@ -59,8 +59,7 @@
     far = ctx_count // pair
     near_groups = [[f * pair + p for p in range(pair)] for f in range(far)]
     far_groups = [[f * pair + p for f in range(far)] for p in range(pair)]
-    held = partial.reshape(batch_count, far, pair, own_rows, columns)
-    held = jnp.transpose(held, (2, 0, 1, 3, 4))
+    held = partial.reshape(pair, batch_count, far, own_rows, columns)
     if pair > 1:
         held = exchange(held, "ctx", near_groups)
     held = fold(held)
@@ -172,6 +171,12 @@
             dispatch, back.reshape(slot_total, model_width), preferred_element_type=jnp.float32
         )
 
+    pair = 2 if ctx_count % 2 == 0 else 1
+
+    def paired(features):
+        blocks = features.reshape(-1, batch_count, ctx_count // pair, pair, own_rows)
+        return jnp.transpose(blocks, (0, 3, 1, 2, 4)).reshape(-1, model_width)
+
     seg_columns = cdiv(tok_rows, own_rows)
     seg_pad = jnp.pad(seg_local, (0, seg_columns * own_rows - tok_rows))
     small_width = experts + 2 + seg_columns
@@ -191,6 +196,8 @@
         axis=1,
     )
     dense_full = lax.all_gather(dense_own, ("batch", "ctx"), axis=0, tiled=True)
+    grad_rows_moe = send_tokens(grad_wire)
+    dense_full, grad_rows_moe = lax.optimization_barrier((dense_full, grad_rows_moe))
     qkv_width = query_width + 2 * kv_width
     qkv_full = dense_full[:, :qkv_width]
     output_full = dense_full[:, qkv_width : qkv_width + model_width]
@@ -215,7 +222,6 @@
         expert_full = lax.all_gather(expert_own, "batch", axis=1, tiled=True)
     gate_up_full = expert_full[:, :, : 2 * unit_count]
     down_full = expert_full[:, :, 2 * unit_count :]
-    grad_rows_moe = send_tokens(grad_wire)
 
     positions = ctx_index * tok_rows + jnp.arange(tok_rows, dtype=jnp.int32)
     cos_table, sin_table = rope_tables(positions, HEAD_DIM)
@@ -260,48 +266,56 @@
     up_pre = gate_up[..., unit_count:]
     sigmoid_gate = jax.nn.sigmoid(gate_pre)
     silu_gate = gate_pre * sigmoid_gate
-    hidden_act = (silu_gate * up_pre).astype(jnp.bfloat16)
-    expert_out = jnp.einsum(
-        "gesf,edf->gesd", hidden_act, down_full, preferred_element_type=jnp.float32
-    )
-    grad_rows_wide = grad_rows_moe.astype(jnp.float32)
-    grad_dots = jnp.sum(grad_rows_wide * expert_out, axis=-1)
+    hidden_act = silu_gate * up_pre
+    grad_plain = jnp.einsum(
+        "gesd,edf->gesf", grad_rows_moe, down_full, preferred_element_type=jnp.float32
+    )
+    grad_dots = jnp.sum(grad_plain * hidden_act, axis=-1)
     dots_back = exchange(grad_dots.reshape(experts, CAP), token_axes)
-    grad_slots = (weight_arrived * grad_rows_wide).astype(jnp.bfloat16)
-    grad_hidden = jnp.einsum(
-        "gesd,edf->gesf", grad_slots, down_full, preferred_element_type=jnp.float32
-    )
+    hidden_weighted = (weight_arrived * hidden_act).astype(jnp.bfloat16)
+    grad_hidden = weight_arrived * grad_plain
     grad_gate = grad_hidden * up_pre * sigmoid_gate * (1.0 + gate_pre * (1.0 - sigmoid_gate))
     grad_up = grad_hidden * silu_gate
-    grad_gate_up = jnp.concatenate([grad_gate, grad_up], axis=-1).astype(jnp.bfloat16)
+    grad_gate = grad_gate.astype(jnp.bfloat16)
+    grad_up = grad_up.astype(jnp.bfloat16)
     grad_expert_in = jnp.einsum(
-        "gesf,edf->gesd", grad_gate_up, gate_up_full, preferred_element_type=jnp.float32
+        "gesf,edf->gesd",
+        jnp.concatenate([grad_gate, grad_up], axis=-1),
+        gate_up_full,
+        preferred_element_type=jnp.float32,
     ).astype(jnp.bfloat16)
     grad_from_experts = return_tokens(grad_expert_in)
-    grad_w_gate_up = jnp.einsum(
-        "gesd,gesf->edf", arrived, grad_gate_up, preferred_element_type=jnp.float32
-    )
-    grad_w_down = jnp.einsum(
-        "gesd,gesf->edf", grad_slots, hidden_act, preferred_element_type=jnp.float32
-    )
-    grad_experts = jnp.concatenate([grad_w_gate_up, grad_w_down], axis=2).astype(jnp.bfloat16)
-    weighted_out = (weight_arrived * expert_out).astype(jnp.bfloat16)
+    grad_experts = jnp.concatenate(
+        [
+            jnp.einsum("gesd,gesf->edf", rows, units, preferred_element_type=jnp.float32).astype(
+                jnp.bfloat16
+            )
+            for rows, units in (
+                (arrived, grad_gate),
+                (arrived, grad_up),
+                (grad_rows_moe, hidden_weighted),
+            )
+        ],
+        axis=0,
+    )
     if spread:
         expert_sum = lax.all_to_all(
             grad_experts, "batch", split_axis=1, concat_axis=0, tiled=True
         )
     else:
         expert_sum = lax.psum_scatter(grad_experts, "batch", scatter_dimension=1, tiled=True)
-    expert_sum = expert_sum.astype(jnp.float32)
+    expert_sum = expert_sum.reshape(-1, 3, served, expert_sum.shape[1], unit_count)
+    weighted_out = jnp.einsum(
+        "gesf,edf->gesd", hidden_weighted, down_full, preferred_element_type=jnp.float32
+    ).astype(jnp.bfloat16)
     moe_out = return_tokens(weighted_out)
-    block_out = (hidden_res + moe_out).astype(jnp.bfloat16)
 
     grad_weights = jnp.sum(jnp.where(slot_mask, dots_back[None], 0.0), axis=-1)
     grad_chosen = route_weights * (
         grad_weights - jnp.sum(route_weights * grad_weights, axis=-1, keepdims=True)
     )
     grad_logits = grad_chosen.astype(jnp.bfloat16)
-    grad_router = jnp.dot(normed_moe.T, grad_logits, preferred_element_type=jnp.float32)
+    grad_router = jnp.dot(paired(normed_moe).T, grad_logits, preferred_element_type=jnp.float32)
     grad_normed = (
         jnp.dot(grad_logits, router_full.T, preferred_element_type=jnp.float32)
         + grad_from_experts
@@ -314,21 +328,7 @@
         - hidden_res * inv_second**3 * jnp.mean(gained_moe * hidden_res, axis=-1, keepdims=True)
     )
     grad_attn = grad_hidden_res.astype(jnp.bfloat16)
-    grad_w_output = jnp.dot(attn_flat.T, grad_attn, preferred_element_type=jnp.float32)
-    tail_pad = cdiv(experts + 1, 128) * 128 - experts - 1
-    first_sum = scatter_sum(
-        jnp.concatenate(
-            [
-                grad_w_output,
-                grad_router,
-                grad_gain_moe[:, None],
-                jnp.zeros((model_width, tail_pad), jnp.float32),
-            ],
-            axis=1,
-        ).astype(jnp.bfloat16),
-        batch_count,
-        ctx_count,
-    )
+    grad_w_output = jnp.dot(paired(attn_flat).T, grad_attn, preferred_element_type=jnp.float32)
 
     grad_attn_rows = (
         jnp.dot(grad_attn, output_full.T, preferred_element_type=jnp.float32)
@@ -339,14 +339,21 @@
         grad_attn_rows.astype(jnp.float32) * attn_rows.astype(jnp.float32), axis=-1
     )
     query_all = lax.all_gather(query_rot.reshape(tok_rows, query_width), "ctx", axis=0, tiled=True)
-    grad_rows_all = lax.all_gather(
-        grad_attn_rows.reshape(tok_rows, query_width), "ctx", axis=0, tiled=True
-    )
-    stats_all = lax.all_gather(
+    stats = jnp.concatenate(
+        [
+            jnp.transpose(log_totals[..., 0], (2, 0, 1)).reshape(tok_rows, HEADS),
+            delta_rows.reshape(tok_rows, HEADS),
+        ],
+        axis=1,
+    )
+    stats_high = lax.reduce_precision(stats, 8, 7)
+    stats_pieces = jnp.concatenate([stats_high, stats - stats_high], axis=1).astype(jnp.bfloat16)
+    back_all = lax.all_gather(
         jnp.concatenate(
             [
-                jnp.transpose(log_totals[..., 0], (2, 0, 1)).reshape(tok_rows, HEADS),
-                delta_rows.reshape(tok_rows, HEADS),
+                grad_attn_rows.reshape(tok_rows, query_width),
+                stats_pieces,
+                jnp.zeros((tok_rows, -4 * HEADS % 128), jnp.bfloat16),
             ],
             axis=1,
         ),
@@ -354,6 +361,9 @@
         axis=0,
         tiled=True,
     )
+    grad_rows_all = back_all[:, :query_width]
+    pieces_all = back_all[:, query_width : query_width + 4 * HEADS].astype(jnp.float32)
+    stats_all = pieces_all[:, : 2 * HEADS] + pieces_all[:, 2 * HEADS :]
     prob_wire, grad_score = score_grads(
         query_groups,
         key_heads,
@@ -404,7 +414,9 @@
         ],
         axis=1,
     ).astype(jnp.bfloat16)
-    grad_w_qkv = jnp.dot(normed_attn.T, grad_qkv, preferred_element_type=jnp.float32)
+    grad_qkv, moe_out = lax.optimization_barrier((grad_qkv, moe_out))
+    block_out = (hidden_res + moe_out).astype(jnp.bfloat16)
+    grad_w_qkv = jnp.dot(paired(normed_attn).T, grad_qkv, preferred_element_type=jnp.float32)
     grad_normed_attn = jnp.dot(grad_qkv, qkv_full.T, preferred_element_type=jnp.float32)
     gained_attn = grad_normed_attn * gain_attn
     grad_gain_attn = jnp.sum(grad_normed_attn * residual_in * inv_first, axis=0)
@@ -413,34 +425,41 @@
         + inv_first * gained_attn
         - residual_in * inv_first**3 * jnp.mean(gained_attn * residual_in, axis=-1, keepdims=True)
     )
-    last_sum = scatter_sum(
-        jnp.concatenate(
+    gains = paired(jnp.stack([grad_gain_attn, grad_gain_moe])).T
+    dense_partial, expert_sum = lax.optimization_barrier(
+        (jnp.concatenate(
             [
-                grad_w_qkv,
-                grad_gain_attn[:, None],
-                jnp.zeros((model_width, 127), jnp.float32),
+                grad_w_qkv.astype(jnp.bfloat16),
+                grad_w_output.astype(jnp.bfloat16),
+                grad_router.astype(jnp.bfloat16),
+                gains.astype(jnp.bfloat16),
+                jnp.zeros((model_width, -(experts + 2) % 128), jnp.bfloat16),
             ],
             axis=1,
-        ).astype(jnp.bfloat16),
-        batch_count,
-        ctx_count,
-    )
-    router_sum = first_sum[:, model_width : model_width + experts]
+        ), expert_sum)
+    )
+    dense_sum = scatter_sum(dense_partial, batch_count, ctx_count)
+    small_sum = dense_sum[:, qkv_width + model_width :]
+    router_sum = small_sum[:, :experts]
     if spread:
         router_sum = router_sum[:, jnp.array(place, dtype=jnp.int32)]
+
+    def own_experts(kind):
+        return expert_sum[:, kind].reshape(w_gate.shape).astype(jnp.float32)
+
     return (
         block_out[None],
         grad_inputs[None],
-        last_sum[:, :query_width],
-        last_sum[:, query_width : query_width + kv_width],
-        last_sum[:, query_width + kv_width : qkv_width],
-        first_sum[:, :model_width],
+        dense_sum[:, :query_width],
+        dense_sum[:, query_width : query_width + kv_width],
+        dense_sum[:, query_width + kv_width : qkv_width],
+        dense_sum[:, qkv_width : qkv_width + model_width],
         router_sum,
-        last_sum[:, qkv_width],
-        first_sum[:, model_width + experts],
-        expert_sum[:, :, :unit_count],
-        expert_sum[:, :, unit_count : 2 * unit_count],
-        expert_sum[:, :, 2 * unit_count :],
+        small_sum[:, experts],
+        small_sum[:, experts + 1],
+        own_experts(0),
+        own_experts(1),
+        own_experts(2),
     )
 
 

time: 727 us -> 717 us (0.986)
  waiting for transfers between devices: 312 us -> 404 us
  local copies, waits for them, and re-layouts: 95.3 us -> 48.7 us
  other arithmetic: 59.7 us -> 35.3 us
  blocking collectives: 91.2 us -> 67.3 us
  starting transfers between devices: 43.3 us -> 35.1 us
    all_to_all x9 -> x6, waiting for transfers between devices: 213 us -> 346 us  [exchange(): lax.all_to_all(blocks, axis, split_axis=0, concat_axis=0, axis_index_grou...]
    all_gather x1, waiting for transfers between devices: 70.8 us -> 0.01 us  [shards(): dense_full = lax.all_gather(dense_own, ('batch', 'ctx'), axis=0, tiled=True)]
    all_gather x1 -> x0, blocking collectives: 63 us -> none  [shards(): lax.all_gather(jnp.concatenate([jnp.transpose(log_totals[..., 0], (2, 0,...]
    all_to_all x3, blocking collectives: 28.1 us -> 67.3 us  [exchange(): lax.all_to_all(blocks, axis, split_axis=0, concat_axis=0, axis_index_grou...]
    all_to_all x1, waiting for transfers between devices: 13.3 us -> 40.1 us  [shards(): lax.all_to_all(grad_experts, 'batch', split_axis=1, concat_axis=0, tiled=...]
    unnamed x119 -> x99, local copies, waits for them, and re-layouts: 26.9 us -> 3.15 us
    unnamed x1 -> x0, other arithmetic: 20.3 us -> none
    all_to_all x9 -> x6, starting transfers between devices: 34.2 us -> 25.1 us  [exchange(): lax.all_to_all(blocks, axis, split_axis=0, concat_axis=0, axis_index_grou...]
  transfers between devices with their start and end apart: 15 -> 12, of which waited for: 10 -> 9; matrix products, arithmetic and copies ran while one was open for 30% -> 11% of each run, Pallas kernels for 0% -> 0%
where the time goes in v2:
time: 717 us; the launch traced here: 707 us
  waiting for transfers between devices  404 us (56%)
  matrix products  101 us (14%)
  blocking collectives  67.3 us (9%)
  local copies, waits for them, and re-layouts  48.7 us (7%)
  other arithmetic  35.3 us (5%)
  starting transfers between devices  35.1 us (5%)
  between operations  15.1 us (2%)
    all_to_all x6, waiting for transfers between devices, exchange(): lax.all_to_all(blocks, axis, split_axis=0, concat_axis=0, axis_index_grou...  346 us
    all_to_all x3, blocking collectives, exchange(): lax.all_to_all(blocks, axis, split_axis=0, concat_axis=0, axis_index_grou...  67.3 us
    all_to_all x1, waiting for transfers between devices, shards(): lax.all_to_all(grad_experts, 'batch', split_axis=1, concat_axis=0, tiled=...  40.1 us
    all_to_all x6, starting transfers between devices, exchange(): lax.all_to_all(blocks, axis, split_axis=0, concat_axis=0, axis_index_grou...  25.1 us
    all_gather x1, waiting for transfers between devices, shards(): lax.all_gather(jnp.concatenate([key_rot.reshape(tok_rows, kv_width), valu...  16.5 us
  transfers between devices with their start and end apart: 12, of which 9 were waited for; matrix products, arithmetic and copies ran while one was open for 11% of the time, Pallas kernels for 0%

profile of v2, /device:TPU:0, one launch (start us, length us, event | category | flops | bytes accessed | tf_op | source)
XLA Modules:
  0.0 707.1 jit_solution(7793981108808211062)
XLA Ops:
  18.1 7.3 %all-to-all-start = ((bf16[32,48,1024]{2,1,0:T(8,128)(2,1)}), bf16[32,48,1024]{2,1,0:T(8,128)(2,1)S(1)}, u32[]{:S(2)}, u32[]{:S(2)}) async-start(bf16[32,48,1024]{2,1,0:T(8,128)(2,1)} %bitcast.7), calls=%async_computation | async-start | bytes 6291456 | tf_op jit(solution)/shard_map/all_to_all | solution.py:46
  26.9 101.8 %all-to-all-done = bf16[32,48,1024]{2,1,0:T(8,128)(2,1)S(1)} async-done(((bf16[32,48,1024]{2,1,0:T(8,128)(2,1)}), bf16[32,48,1024]{2,1,0:T(8,128)(2,1)S(1)}, u32[]{:S(2)}, u32[]{:S(2)}) %all-to-all-start) | async-done | bytes 3145760 | tf_op jit(solution)/shard_map/all_to_all | solution.py:46
  140.0 4.8 all-to-all-start.1
  146.9 16.5 %all-gather.7.cloned.1.call-done = bf16[1024,1024]{1,0:T(8,128)(2,1)} async-done(((bf16[128,1024]{1,0:T(8,128)(2,1)}), bf16[1024,1024]{1,0:T(8,128)(2,1)}) %all-gather.7.cloned.1.call-update) | async-done | bytes 2097168 | tf_op jit(solution)/shard_map/all_gather | solution.py:239
  180.8 3.7 all-to-all-start.2
  185.7 71.3 %all-to-all-done.2 = bf16[32,48,1024]{2,1,0:T(8,128)(2,1)} async-done(((bf16[32,48,1024]{2,1,0:T(8,128)(2,1)}), bf16[32,48,1024]{2,1,0:T(8,128)(2,1)}, u32[]{:S(2)}, u32[]{:S(2)}) %all-to-all-start.2) | async-done | bytes 3145760 | tf_op jit(solution)/shard_map/all_to_all | solution.py:46
  257.1 6.2 convolution_bitcast_fusion
  263.2 6.8 fusion.34
  272.7 7.1 %all-to-all-done.3 = f32[32,1,48]{2,1,0:T(1,128)S(1)} async-done(((f32[32,1,48]{2,1,0:T(1,128)}), f32[32,1,48]{2,1,0:T(1,128)S(1)}, u32[]{:S(2)}, u32[]{:S(2)}) %all-to-all-start.3) | async-done | bytes 6176 | tf_op jit(solution)/shard_map/all_to_all | solution.py:46
  280.4 9.3 %all_to_all.80 = f32[32,1,48]{2,1,0:T(1,128)S(1)} all-to-all(f32[32,1,48]{2,1,0:T(1,128)S(1)} %bitcast.363), channel_id=1, replica_groups=mesh['batch'=4,'ctx'=8] {'batch','ctx'}, dimensions={0} | all-to-all | bytes 12288 | tf_op jit(solution)/shard_map/all_to_all | solution.py:46
  289.7 4.8 multiply_convert_fusion.2
  296.4 3.7 fusion.49
  300.1 3.7 fusion.52
  304.2 4.7 copy.213
  308.9 4.8 all-to-all-start.7
  313.7 7.6 %convert_bitcast_fusion.1 = bf16[32,48,1024]{2,1,0:T(8,128)(2,1)} fusion(bf16[32,1,48,512]{3,2,0,1:T(8,128)(2,1)} %copy-done.12, bf16[32,1,48,512]{3,2,0,1:T(8,128)(2,1)} %copy-done.11, bf16[1,1024,1536]{2,1,0:T(8,128)(2,1)} %bitcast.26), kind=kOutput, calls=%fused_computation.53 | convolution fusion | flops 3229089792 | bytes 8388608 | tf_op jit(solution)/shard_map/gesf,edf->gesd/dot_general | solution.py:281
  321.4 40.1 %all-to-all-done.7 = bf16[3,1024,512]{2,0,1:T(4,128)(2,1)} async-done(((bf16[3,1024,512]{2,0,1:T(4,128)(2,1)}), bf16[3,1024,512]{2,0,1:T(4,128)(2,1)}, u32[]{:S(2)}, u32[]{:S(2)}) %all-to-all-start.7) | async-done | bytes 3145760 | tf_op jit(solution)/shard_map/all_to_all | solution.py:302
  365.8 5.2 convert_bitcast_fusion
  371.0 83.4 %all-to-all-done.5 = bf16[32,48,1024]{2,1,0:T(8,128)(2,1)} async-done(((bf16[32,48,1024]{2,1,0:T(8,128)(2,1)}), bf16[32,48,1024]{2,1,0:T(8,128)(2,1)}, u32[]{:S(2)}, u32[]{:S(2)}) %all-to-all-start.5) | async-done | bytes 3145760 | tf_op jit(solution)/shard_map/all_to_all | solution.py:46
  468.7 6.1 fusion.97
  475.8 4.8 copy.230
  481.3 68.1 %all-to-all-done.6 = bf16[32,48,1024]{2,1,0:T(8,128)(2,1)} async-done(((bf16[32,48,1024]{2,1,0:T(8,128)(2,1)}), bf16[32,48,1024]{2,1,0:T(8,128)(2,1)}, u32[]{:S(2)}, u32[]{:S(2)}) %all-to-all-start.6) | async-done | bytes 3145760 | tf_op jit(solution)/shard_map/all_to_all | solution.py:46
  554.8 7.1 %fusion.17 = f32[8,64,2,128]{3,1,2,0:T(8,128)S(1)} fusion(bf16[1024,8,64,1]{0,2,3,1:T(8,128)(2,1)S(1)} %bitcast.344, f32[8,1024,128,2]{2,1,3,0:T(8,128)} %copy-done.47, f32[8,2,128]{2,1,0:T(2,128)S(1)} %bitcast.366, f32[8,2,128]{2,1,0:T(2,128)S(1)} %copy-done.34, pred[128,1024]{0,1:T(8,128)(4,1)S(1)} %copy-done.24, bf16[1024,8,64,1]{0,2,3,1:T(8,128)(2,1)} %bitcast.345, ...), kind=kOutput, calls=%fused_computation.23 | convolution fusion | flops 551550976 | bytes 11419648 | tf_op jit(solution)/shard_map/kgts,skd->tkgd/dot_general | solution.py:377
  568.7 6.5 fusion.71
  575.3 8.3 %fusion.65 = f32[128,8,64]{0,2,1:T(8,128)S(1)} fusion(bf16[1024,8,2,64]{0,3,2,1:T(8,128)(2,1)S(1)} %bitcast.331, f32[8,128,1024,2]{2,1,3,0:T(8,128)} %fusion.97, f32[8,2,1024]{2,1,0:T(2,128)} %bitcast.361, f32[8,2,1024]{2,1,0:T(2,128)S(1)} %bitcast.360, pred[1024,128]{0,1:T(8,128)(4,1)} %fusion.87, bf16[128,8,64,1]{0,2,3,1:T(8,128)(2,1)} %bitcast.356, ...), kind=kOutput, calls=%fused_computation.82 | convolution fusion | flops 551550976 | bytes 13238272 | tf_op jit(solution)/shard_map/kgts,tkgd->skd/dot_general | solution.py:397
  584.7 5.0 fusion.85
  594.2 10.4 %concatenate.54 = bf16[1024,3200]{1,0:T(8,128)(2,1)} concatenate(bf16[1024,2048]{1,0:T(8,128)(2,1)} %convolution_convert_fusion.2, bf16[1024,1024]{1,0:T(8,128)(2,1)S(1)} %copy-done.2, bf16[1024,32]{1,0:T(8,128)(2,1)S(1)} %copy-done.18, bf16[1024,2]{1,0:T(8,128)(2,1)} %bitcast.353, bf16[1024,94]{1,0:T(8,128)(2,1)S(1)} %broadcast_in_dim.138), dimensions={1} | concatenate | bytes 13107200 | tf_op jit(solution)/shard_map/concatenate | solution.py:430
  604.6 15.7 %all_to_all.81 = bf16[2,4,4,32,3200]{4,3,2,1,0:T(8,128)(2,1)} all-to-all(bf16[2,4,4,32,3200]{4,3,2,1,0:T(8,128)(2,1)} %bitcast.327), channel_id=1, replica_groups={{0,1},{2,3},{4,5},{6,7},{8,9},{10,11},{12,13},{14,15},{16,17},{18,19},{..., dimensions={0} | all-to-all | bytes 13107200 | tf_op jit(solution)/shard_map/all_to_all | solution.py:46
  620.3 6.5 reduce_sum.163
  626.8 42.3 %all_to_all.82 = bf16[4,4,32,3200]{3,2,1,0:T(8,128)(2,1)S(1)} all-to-all(bf16[4,4,32,3200]{3,2,1,0:T(8,128)(2,1)} %reduce_sum.163), channel_id=1, replica_groups=mesh['batch'=4,'ctx'=8] {'batch'}, dimensions={0} | all-to-all | bytes 6553600 | tf_op jit(solution)/shard_map/all_to_all | solution.py:46
  670.7 4.5 all-to-all-start.10
  681.5 14.0 %all-to-all-done.10 = bf16[4,32,3200]{2,1,0:T(8,128)(2,1)} async-done(((bf16[4,32,3200]{2,1,0:T(8,128)(2,1)}), bf16[4,32,3200]{2,1,0:T(8,128)(2,1)}, u32[]{:S(2)}, u32[]{:S(2)}) %all-to-all-start.10) | async-done | bytes 819232 | tf_op jit(solution)/shard_map/all_to_all | solution.py:46
  (224 shorter events, 99.7 us)
Async XLA Ops:
  7.2 121.6 %all-gather.5.cloned.1.call-start = ((), (), s32[]{:S(2)}) async-start(), calls=%async_computation.11 | async-start | bytes 6758400 | tf_op jit(solution)/shard_map/all_gather | solution.py:198
  14.1 443.9 %copy-start.19 = (pred[128,32]{0,1:T(8,128)(4,1)}, pred[128,32]{0,1:T(8,128)(4,1)S(1)}, u32[]{:S(2)}) copy-start(pred[128,32]{0,1:T(8,128)(4,1)S(1)} %compare_reduce_fusion) | copy-start | bytes 12292
  18.1 110.7 %all-to-all-start = ((bf16[32,48,1024]{2,1,0:T(8,128)(2,1)}), bf16[32,48,1024]{2,1,0:T(8,128)(2,1)S(1)}, u32[]{:S(2)}, u32[]{:S(2)}) async-start(bf16[32,48,1024]{2,1,0:T(8,128)(2,1)} %bitcast.7), calls=%async_computation | async-start | bytes 6291456 | tf_op jit(solution)/shard_map/all_to_all | solution.py:46
  25.4 138.0 %all-gather.7.cloned.1.call-start = ((), (), s32[]{:S(2)}) async-start(), calls=%async_computation.12 | async-start | bytes 2359296 | tf_op jit(solution)/shard_map/all_gather | solution.py:239
  26.1 107.4 %copy-start.41 = (f32[128]{0:T(128)}, f32[128]{0:T(128)S(1)}, u32[]{:S(2)}) copy-start(f32[128]{0:T(128)S(1)} %get-tuple-element.130) | copy-start | bytes 1540
  26.9 109.1 %copy-start.21 = (f32[128,32]{0,1:T(8,128)}, f32[128,32]{0,1:T(8,128)S(1)}, u32[]{:S(2)}) copy-start(f32[128,32]{0,1:T(8,128)S(1)} %get-tuple-element.128) | copy-start | bytes 49156
  140.0 40.8 %all-to-all-start.1 = ((bf16[4,256,1536]{2,1,0:T(8,128)(2,1)}), bf16[4,256,1536]{2,1,0:T(8,128)(2,1)}, u32[]{:S(2)}, u32[]{:S(2)}) async-start(bf16[4,256,1536]{2,1,0:T(8,128)(2,1)} %pad_maximum_fusion), calls=%async_computation.1 | async-start | bytes 6291456 | tf_op jit(solution)/shard_map/all_to_all | solution.py:218
  145.2 21.2 %copy-start.37 = (s32[128]{0:T(128)}, s32[128]{0:T(128)S(1)}, u32[]{:S(2)}) copy-start(s32[128]{0:T(128)S(1)} %iota_add_fusion) | copy-start | bytes 1540
  145.2 21.2 %copy-start.39 = (bf16[128]{0:T(256)(128)(2,1)}, bf16[128]{0:T(256)(128)(2,1)S(1)}, u32[]{:S(2)}) copy-start(bf16[128]{0:T(256)(128)(2,1)S(1)} %convert_bitcast_fusion.2) | copy-start | bytes 772
  146.7 19.8 %copy-start.35 = (bf16[1024]{0:T(1024)(128)(2,1)}, bf16[1024]{0:T(1024)(128)(2,1)S(1)}, u32[]{:S(2)}) copy-start(bf16[1024]{0:T(1024)(128)(2,1)S(1)} %dynamic-slice_reduce_fusion) | copy-start | bytes 6148
  146.7 21.0 %copy-start.15 = (bf16[128,16,64]{0,2,1:T(8,128)(2,1)}, bf16[128,16,64]{0,2,1:T(8,128)(2,1)S(1)}, u32[]{:S(2)}) copy-start(bf16[128,16,64]{0,2,1:T(8,128)(2,1)S(1)} %pad_maximum_fusion.5) | copy-start | bytes 786436
  146.9 24.1 %copy-start.23 = (pred[128,1024]{0,1:T(8,128)(4,1)}, pred[128,1024]{0,1:T(8,128)(4,1)S(1)}, u32[]{:S(2)}) copy-start(pred[128,1024]{0,1:T(8,128)(4,1)S(1)} %fusion.86) | copy-start | bytes 393220
  176.4 285.6 %copy-start = (f32[128,1024]{1,0:T(8,128)}, f32[128,1024]{1,0:T(8,128)S(1)}, u32[]{:S(2)}) copy-start(f32[128,1024]{1,0:T(8,128)S(1)} %get-tuple-element.136) | copy-start | bytes 1572868
  180.8 76.3 %all-to-all-start.2 = ((bf16[32,48,1024]{2,1,0:T(8,128)(2,1)}), bf16[32,48,1024]{2,1,0:T(8,128)(2,1)}, u32[]{:S(2)}, u32[]{:S(2)}) async-start(bf16[32,48,1024]{2,1,0:T(8,128)(2,1)} %bitcast.329), calls=%async_computation.2 | async-start | bytes 6291456 | tf_op jit(solution)/shard_map/all_to_all | solution.py:46
  270.1 9.6 %all-to-all-start.3 = ((f32[32,1,48]{2,1,0:T(1,128)}), f32[32,1,48]{2,1,0:T(1,128)S(1)}, u32[]{:S(2)}, u32[]{:S(2)}) async-start(f32[32,1,48]{2,1,0:T(1,128)} %bitcast.40), calls=%async_computation.3 | async-start | bytes 32768 | tf_op jit(solution)/shard_map/all_to_all | solution.py:46
  308.9 52.6 %all-to-all-start.7 = ((bf16[3,1024,512]{2,0,1:T(4,128)(2,1)}), bf16[3,1024,512]{2,0,1:T(4,128)(2,1)}, u32[]{:S(2)}, u32[]{:S(2)}) async-start(bf16[3,1024,512]{2,0,1:T(4,128)(2,1)} %copy.213), calls=%async_computation.7 | async-start | bytes 8388608 | tf_op jit(solution)/shard_map/all_to_all | solution.py:302
  361.5 92.9 %all-to-all-start.5 = ((bf16[32,48,1024]{2,1,0:T(8,128)(2,1)}), bf16[32,48,1024]{2,1,0:T(8,128)(2,1)}, u32[]{:S(2)}, u32[]{:S(2)}) async-start(bf16[32,48,1024]{2,1,0:T(8,128)(2,1)} %convert_bitcast_fusion.1), calls=%async_computation.5 | async-start | bytes 6291456 | tf_op jit(solution)/shard_map/all_to_all | solution.py:46
  365.0 103.6 %all-gather.9.cloned.1.call-start = ((), (), s32[]{:S(2)}) async-start(), calls=%async_computation.13 | async-start | bytes 2359296 | tf_op jit(solution)/shard_map/all_gather | solution.py:341
  454.4 95.0 %all-to-all-start.6 = ((bf16[32,48,1024]{2,1,0:T(8,128)(2,1)}), bf16[32,48,1024]{2,1,0:T(8,128)(2,1)}, u32[]{:S(2)}, u32[]{:S(2)}) async-start(bf16[32,48,1024]{2,1,0:T(8,128)(2,1)} %convert_bitcast_fusion), calls=%async_computation.6 | async-start | bytes 6291456 | tf_op jit(solution)/shard_map/all_to_all | solution.py:46
  458.0 103.9 %all-gather.11.cloned.1.call-start = ((), (), s32[]{:S(2)}) async-start(), calls=%async_computation.14 | async-start | bytes 2654208 | tf_op jit(solution)/shard_map/all_gather | solution.py:351
  462.2 90.5 %copy-start.5 = (f32[128,1024]{1,0:T(8,128)}, f32[128,1024]{1,0:T(8,128)S(1)}, u32[]{:S(2)}) copy-start(f32[128,1024]{1,0:T(8,128)S(1)} %multiply_subtract_fusion) | copy-start | bytes 1572868
  465.2 9.6 %copy-start.30 = (f32[128,8,2]{0,2,1:T(2,128)}, f32[128,8,2]{0,2,1:T(2,128)S(1)}, u32[]{:S(2)}) copy-start(f32[128,8,2]{0,2,1:T(2,128)S(1)} %multiply_reduce_fusion.1) | copy-start | bytes 24580
  475.8 73.6 %copy-start.20 = (pred[128,32]{0,1:T(8,128)(4,1)S(1)}, pred[128,32]{0,1:T(8,128)(4,1)}, u32[]{:S(2)}) copy-start(pred[128,32]{0,1:T(8,128)(4,1)} %copy-done.19) | copy-start | bytes 12292
  481.3 73.5 %copy-start.13 = (bf16[1024,512]{0,1:T(8,128)(2,1)S(1)}, bf16[1024,512]{0,1:T(8,128)(2,1)}, u32[]{:S(2)}) copy-start(bf16[1024,512]{0,1:T(8,128)(2,1)} %copy.193) | copy-start | bytes 3145732
  481.3 73.5 %copy-start.24 = (pred[128,1024]{0,1:T(8,128)(4,1)S(1)}, pred[128,1024]{0,1:T(8,128)(4,1)}, u32[]{:S(2)}) copy-start(pred[128,1024]{0,1:T(8,128)(4,1)} %copy-done.23) | copy-start | bytes 393220
  481.3 73.5 %copy-start.31 = (f32[128,8,2]{0,2,1:T(2,128)S(1)}, f32[128,8,2]{0,2,1:T(2,128)}, u32[]{:S(2)}) copy-start(f32[128,8,2]{0,2,1:T(2,128)} %copy-done.30) | copy-start | bytes 24580
  481.3 73.5 %copy-start.34 = (f32[8,2,128]{2,1,0:T(2,128)S(1)}, f32[8,2,128]{2,1,0:T(2,128)}, u32[]{:S(2)}) copy-start(f32[8,2,128]{2,1,0:T(2,128)} %copy-done.33) | copy-start | bytes 24580
  575.2 8.3 %copy-start.22 = (f32[128,32]{0,1:T(8,128)S(1)}, f32[128,32]{0,1:T(8,128)}, u32[]{:S(2)}) copy-start(f32[128,32]{0,1:T(8,128)} %copy-done.21) | copy-start | bytes 49156
  575.2 8.3 %copy-start.26 = (f32[128,32]{0,1:T(8,128)S(1)}, f32[128,32]{0,1:T(8,128)}, u32[]{:S(2)}) copy-start(f32[128,32]{0,1:T(8,128)} %get-tuple-element.126) | copy-start | bytes 49156
  575.2 9.4 %copy-start.29 = (f32[1024]{0:T(1024)S(1)}, f32[1024]{0:T(1024)}, u32[]{:S(2)}) copy-start(f32[1024]{0:T(1024)} %copy-done.27) | copy-start | bytes 12292
  575.2 9.4 %copy-start.43 = (f32[128]{0:T(128)S(1)}, f32[128]{0:T(128)}, u32[]{:S(2)}) copy-start(f32[128]{0:T(128)} %copy-done.41) | copy-start | bytes 1540
  670.7 24.7 %all-to-all-start.10 = ((bf16[4,32,3200]{2,1,0:T(8,128)(2,1)}), bf16[4,32,3200]{2,1,0:T(8,128)(2,1)}, u32[]{:S(2)}, u32[]{:S(2)}) async-start(bf16[4,32,3200]{2,1,0:T(8,128)(2,1)} %reduce_sum.164), calls=%async_computation.10 | async-start | bytes 1638400 | tf_op jit(solution)/shard_map/all_to_all | solution.py:46
  (29 other events, 140.0 us)
Sparse Core Ops, SparseCore 0:
  13.5 104.9 all-gather.4
  137.1 26.2 all-gather.6
  367.4 59.5 all-gather.8
  466.4 60.5 all-gather.10
